TPU v7x, 32 devices: a whole 2x2x4 slice. The times are simulated.
32 devices in a mesh: node: 8 (over z, x), feat: 4 (over y, core).
Axes of the slice: x: 2, y: 2, z: 4, core: 2. Of those that a mesh axis runs over, the one named last changes fastest.
Arguments:
- feature_table: bfloat16 [8192, 2048], P('node', 'feat'), may hold values from -6 to 6
- hub_table: bfloat16 [32, 2048], P('node', 'feat'), may hold values from -6 to 6
- first_self: bfloat16 [2048, 2048], P('feat'), may hold values from -0.125 to 0.125
- first_pooled: bfloat16 [2048, 2048], P('feat'), may hold values from -0.125 to 0.125
- second_self: bfloat16 [2048, 256], P('feat'), may hold values from -0.125 to 0.125
- second_pooled: bfloat16 [2048, 256], P('feat'), may hold values from -0.125 to 0.125
- first_lists: int32 [3072, 10], P('node'), may hold values from 0 to 8223, as said below
- first_counts: int32 [3072], P('node'), may hold values from 1 to 10
- second_lists: int32 [2048, 5], P('node'), may hold values from 0 to 3071, as said below
- second_counts: int32 [2048], P('node'), may hold values from 1 to 5
Outputs:
- embedding: bfloat16 [2048, 256], P(('node', 'feat'))
Inputs may be any that keep to these rules, and one draw needn't show every extreme that they name: `first_lists`: an entry below 8192 names a row of feature_table, held by node shard (entry // 1024); an entry v of 8192 or more names hub clip v - 8192, owned by node shard (v - 8192) // 4. Slots at or beyond a clip's count are padding and still hold such entries. Of the 3840 entries of one node shard's rows, padding included, at most 480 name feature rows held by any one node shard; in every draw one node shard is named exactly 480 times by the rows of every node shard. `second_lists`: entries name frontier clips, held by node shard (entry // 384). Of the 1280 entries of one node shard's rows, padding included, exactly 160 name frontier clips of each node shard.
All inputs are finite; a program needn't handle non-finite values.
Results may differ from a plain program's by a relative error of at most 0.0052.
Values may be sent and summed in bfloat16 or wider, within the bound.
A program may use at most 64 MiB of HBM per device.

v0:
```python
import jax
import jax.numpy as jnp
from jax import lax
from jax.sharding import PartitionSpec as P


def slot_positions(owners, shards, capacity):
    columns = jnp.arange(shards, dtype=jnp.int32)
    onehot = (owners[:, None] == columns[None, :]).astype(jnp.int32)
    earlier = jnp.cumsum(onehot, axis=0) - onehot
    ranking = jnp.sum(earlier * onehot, axis=1)
    return jnp.where(owners >= 0, owners * capacity + ranking, shards * capacity)


def build_requests(local_index, position, shards, capacity):
    request = jnp.zeros((shards * capacity,), jnp.int32)
    request = request.at[position].set(local_index, mode="drop")
    return request.reshape(shards, capacity)


def masked_mean(picked, counts, fanout):
    valid = jnp.arange(fanout, dtype=jnp.int32)[None, :] < counts[:, None]
    summed = jnp.sum(jnp.where(valid[:, :, None], picked.astype(jnp.float32), 0.0), axis=1)
    return (summed / counts[:, None].astype(jnp.float32)).astype(jnp.bfloat16)


def body(
    feature_table,
    hub_table,
    first_self,
    first_pooled,
    second_self,
    second_pooled,
    first_lists,
    first_counts,
    second_lists,
    second_counts,
):
    shards = lax.axis_size("node")
    rows_here = feature_table.shape[0]
    hubs_here = hub_table.shape[0]
    front_here, fanout_one = first_lists.shape
    targets_here, fanout_two = second_lists.shape
    width_part = feature_table.shape[1]
    total_rows = rows_here * shards
    entries = first_lists.reshape(-1)
    is_hub = entries >= total_rows
    stride = rows_here + hubs_here
    hub_index = entries - total_rows
    merged = jnp.where(
        is_hub,
        hub_index // hubs_here * stride + rows_here + hub_index % hubs_here,
        entries // rows_here * stride + entries % rows_here,
    )
    combined = jnp.concatenate([feature_table, hub_table], axis=0)
    whole_table = lax.all_gather(combined, "node", axis=0, tiled=True)
    picked = jnp.take(whole_table, merged, axis=0)
    first_mean = masked_mean(
        picked.reshape(front_here, fanout_one, width_part), first_counts, fanout_one
    )
    own_rows = feature_table[:front_here]
    partial_value = jnp.dot(own_rows, first_self, preferred_element_type=jnp.float32)
    partial_value = partial_value + jnp.dot(
        first_mean, first_pooled, preferred_element_type=jnp.float32
    )
    hidden = jax.nn.relu(
        lax.psum_scatter(partial_value, "feat", scatter_dimension=1, tiled=True)
    ).astype(jnp.bfloat16)
    hidden_part = hidden.shape[1]
    named = second_lists.reshape(-1)
    capacity_two = named.shape[0] // shards
    position_two = slot_positions(named // front_here, shards, capacity_two)
    request_two = build_requests(named % front_here, position_two, shards, capacity_two)
    found = jnp.take(
        hidden, lax.all_to_all(request_two, "node", split_axis=0, concat_axis=0, tiled=True), axis=0
    )
    replies_two = lax.all_to_all(found, "node", split_axis=0, concat_axis=0, tiled=True)
    replies_two = replies_two.reshape(shards * capacity_two, hidden_part)
    picked_two = jnp.take(replies_two, jnp.clip(position_two, 0, shards * capacity_two - 1), axis=0)
    second_mean = masked_mean(
        picked_two.reshape(targets_here, fanout_two, hidden_part), second_counts, fanout_two
    )
    own_hidden = hidden[:targets_here]
    mixed_part = jnp.dot(own_hidden, second_self, preferred_element_type=jnp.float32)
    mixed_part = mixed_part + jnp.dot(
        second_mean, second_pooled, preferred_element_type=jnp.float32
    )
    mixed = lax.psum_scatter(mixed_part, "feat", scatter_dimension=0, tiled=True)
    scale = lax.rsqrt(jnp.mean(mixed * mixed, axis=1, keepdims=True) + 1e-06)
    return (mixed * scale).astype(jnp.bfloat16)


def solution(mesh):
    return jax.shard_map(
        body,
        mesh=mesh,
        in_specs=(
            P("node", "feat"),
            P("node", "feat"),
            P("feat", None),
            P("feat", None),
            P("feat", None),
            P("feat", None),
            P("node", None),
            P("node"),
            P("node", None),
            P("node"),
        ),
        out_specs=P(("node", "feat"), None),
        check_vma=False,
    )
```

profile of v0, /device:TPU:0, one launch (start us, length us, event | category | flops | bytes accessed | tf_op | source)
XLA Modules:
  0.0 304.0 jit_solution(17437129462587528165)
XLA Ops:
  6.6 2.4 maximum_bitcast_fusion
  10.2 2.7 fusion.1
  12.8 124.7 %all-gather.3.cloned.1.call-done = bf16[8,1028,512]{2,1,0:T(8,128)(2,1)} async-done(((bf16[1,1028,512]{2,1,0:T(8,128)(2,1)}), bf16[8,1028,512]{2,1,0:T(8,128)(2,1)}) %all-gather.3.cloned.1.call-update) | async-done | bytes 8421392 | tf_op jit(solution)/shard_map/all_gather | solution.py:56
  137.5 7.6 %reshape.513 = bf16[8224,512]{1,0:T(8,128)(2,1)} reshape(bf16[8,1028,512]{2,1,0:T(8,128)(2,1)} %all-gather.3.cloned.1.call-done) | data formatting | bytes 16842752
  145.1 16.4 %gather_fusion = bf16[3840,512]{1,0:T(8,128)(2,1)} fusion(bf16[8224,512]{1,0:T(8,128)(2,1)} %reshape.513, s32[4096]{0:T(1024)S(1)} %pad_clamp_fusion), kind=kCustom, calls=%fused_computation | custom fusion | bytes 7879680 | tf_op jit(solution)/shard_map/jit(_take)/gather | solution.py:57
  161.5 8.2 %gather.17 = bf16[384,10,512]{2,1,0:T(8,128)(2,1)} reshape(bf16[3840,512]{1,0:T(8,128)(2,1)} %gather_fusion) | data formatting | bytes 7864320 | tf_op jit(solution)/shard_map/jit(_take)/gather | solution.py:57
  169.6 7.6 %select_reduce_fusion = f32[384,512]{1,0:T(8,128)S(1)} fusion(bf16[384,10,512]{2,1,0:T(8,128)(2,1)} %gather.17, pred[384,10]{1,0:T(8,128)(4,1)S(1)} %copy.18, pred[384,10]{1,0:T(8,128)(4,1)S(1)} %iota_compare_fusion), kind=kLoop, calls=%fused_computation.4 | loop fusion | flops 7667712 | bytes 4726272 | tf_op jit(solution)/shard_map/reduce_sum | solution.py:23
  177.2 2.7 convolution_add_fusion
  182.0 2.3 reduce-window.6
  185.4 5.2 %scatter_custom_fusion = s32[1280]{0:T(1024)S(1)} fusion(s32[1280]{0:T(1024)S(1)} %get-tuple-element.6, s32[1280]{0:T(1024)S(1)} %get-tuple-element.11, s32[]{:T(128)} %constant.118.clone.1), kind=kCustom, calls=%fused_computation.99 | custom fusion | bytes 5124 | tf_op jit(solution)/shard_map/scatter | solution.py:17
  190.7 9.1 %all_to_all.20 = s32[8,1,160]{2,1,0:T(1,128)S(1)} all-to-all(s32[8,1,160]{2,1,0:T(1,128)S(1)} %all_to_all.13), channel_id=1, replica_groups=mesh['node'=8,'feat'=4] {'node'}, dimensions={0} | all-to-all | bytes 10240 | tf_op jit(solution)/shard_map/all_to_all | solution.py:75
  200.0 16.1 %reduce-scatter.3.cloned.1.call-done = f32[384,512]{1,0:T(8,128)} async-done(((f32[384,2048]{1,0:T(8,128)}), f32[384,512]{1,0:T(8,128)}) %reduce-scatter.3.cloned.1.call-update) | async-done | bytes 786448 | tf_op jit(solution)/shard_map/reduce_scatter | solution.py:67
  216.1 1.2 maximum_convert_fusion
  217.3 4.7 %gather_fusion.1 = bf16[1280,512]{1,0:T(8,128)(2,1)} fusion(bf16[384,512]{1,0:T(8,128)(2,1)S(1)} %maximum_convert_fusion, s32[2048]{0:T(1024)S(1)} %pad_clamp_fusion.2), kind=kCustom, calls=%fused_computation.1 | custom fusion | bytes 2626560 | tf_op jit(solution)/shard_map/jit(_take)/gather | solution.py:74
  222.0 2.6 broadcast_select_fusion
  224.6 5.6 %all-to-all-start.1 = ((bf16[8,160,512]{2,1,0:T(8,128)(2,1)}), bf16[8,160,512]{2,1,0:T(8,128)(2,1)}, u32[]{:S(2)}, u32[]{:S(2)}) async-start(bf16[8,160,512]{2,1,0:T(8,128)(2,1)} %broadcast_select_fusion), calls=%async_computation.2 | async-start | bytes 2621440 | tf_op jit(solution)/shard_map/all_to_all | solution.py:77
  231.8 29.8 %all-to-all-done.1 = bf16[8,160,512]{2,1,0:T(8,128)(2,1)} async-done(((bf16[8,160,512]{2,1,0:T(8,128)(2,1)}), bf16[8,160,512]{2,1,0:T(8,128)(2,1)}, u32[]{:S(2)}, u32[]{:S(2)}) %all-to-all-start.1) | async-done | bytes 1310752 | tf_op jit(solution)/shard_map/all_to_all | solution.py:77
  261.6 5.6 %gather_fusion.2 = bf16[1280,512]{1,0:T(8,128)(2,1)S(1)} fusion(bf16[1280,512]{1,0:T(8,128)(2,1)} %bitcast.4, s32[2048]{0:T(1024)S(1)} %pad_clamp_fusion.1), kind=kCustom, calls=%fused_computation.2 | custom fusion | bytes 2626560 | tf_op jit(solution)/shard_map/jit(_take)/gather | solution.py:79
  267.2 1.6 gather.20
  268.9 6.8 %select_reduce_fusion.1 = f32[256,512]{1,0:T(8,128)S(1)} fusion(bf16[256,5,512]{2,1,0:T(8,128)(2,1)} %gather.20, pred[256,5]{1,0:T(8,128)(4,1)S(1)} %get-tuple-element.14, pred[256,5]{1,0:T(8,128)(4,1)S(1)} %get-tuple-element.13), kind=kLoop, calls=%fused_computation.5 | loop fusion | flops 2490368 | bytes 1837568 | tf_op jit(solution)/shard_map/reduce_sum | solution.py:23
  275.7 1.0 convolution_add_fusion.1
  276.6 18.3 %reduce-scatter.5.cloned.1.call-done = f32[64,256]{1,0:T(8,128)} async-done(((f32[256,256]{1,0:T(8,128)}), f32[64,256]{1,0:T(8,128)}) %reduce-scatter.5.cloned.1.call-update) | async-done | bytes 65552 | tf_op jit(solution)/shard_map/reduce_scatter | solution.py:88
  295.0 0.9 multiply_reduce_fusion
  295.9 1.5 multiply_convert_fusion
  (65 shorter events, 5.9 us)
Async XLA Ops:
  6.5 3.6 %copy-start = (bf16[512,2048]{1,0:T(8,128)(2,1)S(1)}, bf16[512,2048]{1,0:T(8,128)(2,1)}, u32[]{:S(2)}) copy-start(bf16[512,2048]{1,0:T(8,128)(2,1)} %param.12) | copy-start | bytes 6291460
  6.5 3.6 %copy-start.2 = (bf16[1024,512]{1,0:T(8,128)(2,1)S(1)}, bf16[1024,512]{1,0:T(8,128)(2,1)}, u32[]{:S(2)}) copy-start(bf16[1024,512]{1,0:T(8,128)(2,1)} %param.10) | copy-start | bytes 3145732
  6.5 2.6 copy-start.6
  6.5 3.1 %copy-start.8 = (s32[384]{0:T(512)S(1)}, s32[384]{0:T(512)}, u32[]{:S(2)}) copy-start(s32[384]{0:T(512)} %param.17) | copy-start | bytes 4612
  6.5 131.0 %all-gather.3.cloned.1.call-start = ((), (), s32[]{:S(2)}) async-start(), calls=%async_computation.6 | async-start | bytes 9510912 | tf_op jit(solution)/shard_map/all_gather | solution.py:56
  9.1 207.0 %reduce-scatter.3.cloned.1.call-start = ((), (), s32[]{:S(2)}) async-start(), calls=%async_computation.4 | async-start | bytes 3932160 | tf_op jit(solution)/shard_map/reduce_scatter | solution.py:67
  169.6 7.6 %copy-start.1 = (f32[384,2048]{1,0:T(8,128)S(1)}, f32[384,2048]{1,0:T(8,128)}, u32[]{:S(2)}) copy-start(f32[384,2048]{1,0:T(8,128)} %fusion.1) | copy-start | bytes 9437188
  169.6 7.6 %copy-start.3 = (bf16[512,2048]{1,0:T(8,128)(2,1)S(1)}, bf16[512,2048]{1,0:T(8,128)(2,1)}, u32[]{:S(2)}) copy-start(bf16[512,2048]{1,0:T(8,128)(2,1)} %param.13) | copy-start | bytes 6291460
  179.9 0.7 copy-start.7
  222.0 8.7 %copy-start.9 = (s32[256]{0:T(256)S(1)}, s32[256]{0:T(256)}, u32[]{:S(2)}) copy-start(s32[256]{0:T(256)} %param.19) | copy-start | bytes 3076
  224.6 6.3 %copy-start.4 = (bf16[512,256]{1,0:T(8,128)(2,1)S(1)}, bf16[512,256]{1,0:T(8,128)(2,1)}, u32[]{:S(2)}) copy-start(bf16[512,256]{1,0:T(8,128)(2,1)} %param.14) | copy-start | bytes 786436
  224.6 37.0 %all-to-all-start.1 = ((bf16[8,160,512]{2,1,0:T(8,128)(2,1)}), bf16[8,160,512]{2,1,0:T(8,128)(2,1)}, u32[]{:S(2)}, u32[]{:S(2)}) async-start(bf16[8,160,512]{2,1,0:T(8,128)(2,1)} %broadcast_select_fusion), calls=%async_computation.2 | async-start | bytes 2621440 | tf_op jit(solution)/shard_map/all_to_all | solution.py:77
  230.3 64.7 %reduce-scatter.5.cloned.1.call-start = ((), (), s32[]{:S(2)}) async-start(), calls=%async_computation.5 | async-start | bytes 327680 | tf_op jit(solution)/shard_map/reduce_scatter | solution.py:88
  268.9 6.8 %copy-start.5 = (f32[256,256]{1,0:T(8,128)S(1)}, f32[256,256]{1,0:T(8,128)}, u32[]{:S(2)}) copy-start(f32[256,256]{1,0:T(8,128)} %fusion.3) | copy-start | bytes 786436
  268.9 6.8 %copy-start.10 = (bf16[512,256]{1,0:T(8,128)(2,1)S(1)}, bf16[512,256]{1,0:T(8,128)(2,1)}, u32[]{:S(2)}) copy-start(bf16[512,256]{1,0:T(8,128)(2,1)} %param.15) | copy-start | bytes 786436
Sparse Core Ops, SparseCore 0:
  9.5 127.9 all-gather.2
  180.1 35.9 reduce-scatter.2
  276.8 18.1 reduce-scatter.4
where the time goes:
time: 305 us; the launch traced here: 304 us
  waiting for transfers between devices  189 us (62%)
  local copies, waits for them, and re-layouts  52.7 us (17%)
  other arithmetic  26.6 us (9%)
  between operations  13.4 us (4%)
  blocking collectives  9.11 us (3%)
  matrix products  7.27 us (2%)
  starting transfers between devices  5.93 us (2%)
    all_gather x1, waiting for transfers between devices, body(): whole_table = lax.all_gather(combined, 'node', axis=0, tiled=True)  125 us
    all_to_all x1, waiting for transfers between devices, body(): lax.all_to_all(found, 'node', split_axis=0, concat_axis=0, tiled=True)  29.8 us
    gather x2, local copies, waits for them, and re-layouts, body(): picked = jnp.take(whole_table, merged, axis=0)  24.5 us
    reduce_scatter x1, waiting for transfers between devices, body(): lax.psum_scatter(mixed_part, 'feat', scatter_dimension=0, tiled=True)  18.3 us
    reduce_scatter x1, waiting for transfers between devices, body(): lax.psum_scatter(partial_value, 'feat', scatter_dimension=1, tiled=True)  16.1 us
    reduce_sum x2, other arithmetic, masked_mean(): jnp.sum(jnp.where(valid[:, :, None], picked.astype(jnp.float32), 0.0), ax...  14.3 us
    all_to_all x1, blocking collectives, body(): lax.all_to_all(request_two, 'node', split_axis=0, concat_axis=0, tiled=True)  9.11 us
    unnamed x25, local copies, waits for them, and re-layouts  8.53 us
  transfers between devices with their start and end apart: 4, of which 4 were waited for; matrix products, arithmetic and copies ran while one was open for 5% of the time, Pallas kernels for 0%

commit v1 on v0

v1 whole, which is shorter than its diff:
```python
import jax
import jax.numpy as jnp
from jax import lax
from jax.sharding import PartitionSpec as P


def count_matrix(local, width):
    columns = jnp.arange(width, dtype=jnp.int32)[None, :]
    total = jnp.zeros((local.shape[0], width), jnp.float32)
    for k in range(local.shape[1]):
        total = total + (local[:, k : k + 1] == columns).astype(jnp.float32)
    return total.astype(jnp.bfloat16)


def body(
    feature_table,
    hub_table,
    first_self,
    first_pooled,
    second_self,
    second_pooled,
    first_lists,
    first_counts,
    second_lists,
    second_counts,
):
    shards = lax.axis_size("node")
    me = lax.axis_index("node")
    rows_here = feature_table.shape[0]
    hubs_here = hub_table.shape[0]
    front_here, fan_one = first_lists.shape
    targets_here, fan_two = second_lists.shape
    total_rows = rows_here * shards

    slots_one = jnp.arange(fan_one, dtype=jnp.int32)[None, :]
    slots_two = jnp.arange(fan_two, dtype=jnp.int32)[None, :]
    lists_one = jnp.where(slots_one < first_counts[:, None], first_lists, -1)
    lists_two = jnp.where(slots_two < second_counts[:, None], second_lists, -1)
    packed = jnp.concatenate(
        [lists_one.reshape(-1), lists_two.reshape(-1), second_counts]
    ).reshape(1, -1)
    everyone = lax.all_gather(packed, "node", axis=0, tiled=True)
    cut_one = front_here * fan_one
    cut_two = cut_one + targets_here * fan_two
    all_one = everyone[:, :cut_one].reshape(shards * front_here, fan_one)
    all_two = everyone[:, cut_one:cut_two].reshape(shards * targets_here, fan_two)
    all_counts = everyone[:, cut_two:].reshape(shards * targets_here, 1)

    feature_at = all_one - me * rows_here
    hub_at = all_one - total_rows - me * hubs_here
    local_one = jnp.where(
        (feature_at >= 0) & (feature_at < rows_here) & (all_one >= 0),
        feature_at,
        jnp.where((hub_at >= 0) & (hub_at < hubs_here), hub_at + rows_here, -1),
    )
    combined = jnp.concatenate([feature_table, hub_table], axis=0)
    matrix_one = count_matrix(local_one, rows_here + hubs_here)
    sums = jnp.dot(matrix_one, combined, preferred_element_type=jnp.float32)
    sums = lax.psum_scatter(sums.astype(jnp.bfloat16), "node", scatter_dimension=0, tiled=True)
    first_mean = (
        sums.astype(jnp.float32) / first_counts[:, None].astype(jnp.float32)
    ).astype(jnp.bfloat16)

    part = jnp.dot(feature_table[:front_here], first_self, preferred_element_type=jnp.float32)
    part = part + jnp.dot(first_mean, first_pooled, preferred_element_type=jnp.float32)
    hidden = jax.nn.relu(
        lax.psum_scatter(part.astype(jnp.bfloat16), "feat", scatter_dimension=1, tiled=True)
    )

    projected = jnp.dot(hidden, second_pooled, preferred_element_type=jnp.float32)
    own = jnp.dot(hidden[:targets_here], second_self, preferred_element_type=jnp.float32)
    local_two = jnp.where(all_two >= 0, all_two - me * front_here, -1)
    matrix_two = count_matrix(local_two, front_here)
    mixed = jnp.dot(
        matrix_two, projected.astype(jnp.bfloat16), preferred_element_type=jnp.float32
    ) / all_counts.astype(jnp.float32)
    here = lax.dynamic_slice_in_dim(mixed, me * targets_here, targets_here, 0)
    mixed = lax.dynamic_update_slice_in_dim(mixed, here + own, me * targets_here, 0)
    mixed = lax.psum_scatter(mixed, ("node", "feat"), scatter_dimension=0, tiled=True)
    scale = lax.rsqrt(jnp.mean(mixed * mixed, axis=1, keepdims=True) + 1e-06)
    return (mixed * scale).astype(jnp.bfloat16)


def solution(mesh):
    return jax.shard_map(
        body,
        mesh=mesh,
        in_specs=(
            P("node", "feat"),
            P("node", "feat"),
            P("feat", None),
            P("feat", None),
            P("feat", None),
            P("feat", None),
            P("node", None),
            P("node"),
            P("node", None),
            P("node"),
        ),
        out_specs=P(("node", "feat"), None),
        check_vma=False,
    )
```

time: 305 us -> 342 us (1.12)
  waiting for transfers between devices: 189 us -> 233 us
  local copies, waits for them, and re-layouts: 52.7 us -> 20 us
  matrix products: 7.27 us -> 34.4 us
  blocking collectives: 9.11 us -> 32.4 us
  other arithmetic: 26.6 us -> 8.17 us
  starting transfers between devices: 5.93 us -> 0.31 us
    reduce_scatter x2 -> x3, waiting for transfers between devices: 34.4 us -> 233 us  [the longest x1 138 us: body(): lax.psum_scatter(mixed, ('node', 'feat'), scatter_dimension=0, tiled=True)]
    all_gather x1 -> x0, waiting for transfers between devices: 125 us -> none  [body(): whole_table = lax.all_gather(combined, 'node', axis=0, tiled=True)]
    gather x5 -> x0, local copies, waits for them, and re-layouts: 36.5 us -> none  [the longest x2 24.5 us: body(): picked = jnp.take(whole_table, merged, axis=0)]
    all_gather x0 -> x1, blocking collectives: none -> 32.4 us  [body(): everyone = lax.all_gather(packed, 'node', axis=0, tiled=True)]
    all_to_all x1 -> x0, waiting for transfers between devices: 29.8 us -> none  [body(): lax.all_to_all(found, 'node', split_axis=0, concat_axis=0, tiled=True)]
    dot_general x3 -> x4, matrix products: 4.54 us -> 29.6 us  [the longest x1 19.4 us: body(): sums = jnp.dot(matrix_one, combined, preferred_element_type=jnp.float32)]
    reduce_sum x3 -> x0, other arithmetic: 14.4 us -> none  [the longest x2 14.3 us: masked_mean(): jnp.sum(jnp.where(valid[:, :, None], picked.astype(jnp.float32), 0.0), ax...]
    slice x1 -> x2, local copies, waits for them, and re-layouts: 0.29 us -> 10.4 us  [count_matrix(): total = total + (local[:, k:k + 1] == columns).astype(jnp.float32)]
  transfers between devices with their start and end apart: 4 -> 3, of which waited for: 4 -> 3; matrix products, arithmetic and copies ran while one was open for 5% -> 2% of each run, Pallas kernels for 0% -> 0%
where the time goes in v1:
time: 342 us; the launch traced here: 341 us
  waiting for transfers between devices  233 us (68%)
  matrix products  34.4 us (10%)
  blocking collectives  32.4 us (9%)
  local copies, waits for them, and re-layouts  20 us (6%)
  between operations  13.3 us (4%)
  other arithmetic  8.17 us (2%)
    reduce_scatter x1, waiting for transfers between devices, body(): lax.psum_scatter(mixed, ('node', 'feat'), scatter_dimension=0, tiled=True)  138 us
    reduce_scatter x1, waiting for transfers between devices, body(): lax.psum_scatter(sums.astype(jnp.bfloat16), 'node', scatter_dimension=0,...  71.1 us
    all_gather x1, blocking collectives, body(): everyone = lax.all_gather(packed, 'node', axis=0, tiled=True)  32.4 us
    reduce_scatter x1, waiting for transfers between devices, body(): lax.psum_scatter(part.astype(jnp.bfloat16), 'feat', scatter_dimension=1,...  23.5 us
    dot_general x1, matrix products, body(): sums = jnp.dot(matrix_one, combined, preferred_element_type=jnp.float32)  19.4 us
    slice x2, local copies, waits for them, and re-layouts, count_matrix(): total = total + (local[:, k:k + 1] == columns).astype(jnp.float32)  10.4 us
  transfers between devices with their start and end apart: 3, of which 3 were waited for; matrix products, arithmetic and copies ran while one was open for 2% of the time, Pallas kernels for 0%

profile of v1, /device:TPU:0, one launch (start us, length us, event | category | flops | bytes accessed | tf_op | source)
XLA Modules:
  0.0 341.4 jit_solution(16329909199386390386)
XLA Ops:
  6.5 0.9 fusion.27
  7.7 0.7 fusion.25
  8.8 0.7 pad_add_fusion
  9.5 32.4 %all-gather.1 = s32[8,1,5376]{2,1,0:T(1,128)S(1)} all-gather(s32[1,1,5376]{2,1,0:T(1,128)S(1)} %reshape.59), channel_id=2, replica_groups=mesh['node'=8,'feat'=4] {'node'}, dimensions={0}, use_global_device_ids=true | all-gather | bytes 193536 | tf_op jit(solution)/shard_map/all_gather | solution.py:42
  42.0 1.8 ge.24
  43.8 2.8 reshape.57
  46.6 2.8 sub.31
  49.4 2.3 and_select_fusion
  51.7 7.9 %slice_reduce_fusion.9 = (s32[3072]{0:T(1024)S(1)}, s32[3072]{0:T(1024)S(1)}, s32[3072]{0:T(1024)S(1)}, s32[3072]{0:T(1024)S(1)}, s32[3072]{0:T(1024)S(1)}, /*in...) fusion(s32[3072,10]{1,0:T(8,128)S(1)} %and_select_fusion), kind=kLoop, calls=%fused_computation.40 | loop fusion | bytes 245760 | tf_op jit(solution)/shard_map/slice | solution.py:11
  59.7 19.4 %fusion.11 = bf16[3072,512]{1,0:T(8,128)(2,1)} fusion(s32[3072]{0:T(1024)S(1)} %get-tuple-element.6, s32[3072]{0:T(1024)S(1)} %get-tuple-element.7, s32[3072]{0:T(1024)S(1)} %get-tuple-element.8, s32[3072]{0:T(1024)S(1)} %get-tuple-element.9, s32[3072]{0:T(1024)S(1)} %get-tuple-element.10, s32[3072]{0:T(1024)S(1)} %get-tuple-element.11, ...), kind=kOutput, calls=%fused_computation.22 | convolution fusion | flops 3332227072 | bytes 4321280 | tf_op jit(solution)/shard_map/dot_general | solution.py:58
  79.1 0.6 copy-done.3
  79.8 3.6 %fusion.22 = f32[384,2048]{1,0:T(8,128)} fusion(bf16[512,2048]{1,0:T(8,128)(2,1)S(1)} %copy-done, bf16[1024,512]{1,0:T(8,128)(2,1)} %param.10), kind=kOutput, calls=%fused_computation.60 | convolution fusion | flops 805306368 | bytes 5636096 | tf_op jit(solution)/shard_map/dot_general | solution.py:64
  83.4 71.1 %reduce-scatter.4.cloned.1.call-done = bf16[384,512]{1,0:T(8,128)(2,1)} async-done(((bf16[3072,512]{1,0:T(8,128)(2,1)}), bf16[384,512]{1,0:T(8,128)(2,1)}) %reduce-scatter.4.cloned.1.call-update) | async-done | bytes 393232 | tf_op jit(solution)/shard_map/reduce_scatter | solution.py:59
  154.5 4.8 %add_convert_fusion.4 = bf16[384,2048]{1,0:T(8,128)(2,1)} fusion(f32[384,2048]{1,0:T(8,128)} %fusion.22, bf16[512,2048]{1,0:T(8,128)(2,1)} %param.13, bf16[384,512]{1,0:T(8,128)(2,1)} %reduce-scatter.4.cloned.1.call-done, f32[384]{0:T(512)S(1)} %convert_element_type.103), kind=kOutput, calls=%fused_computation.23 | convolution fusion | flops 807469056 | bytes 7210496 | tf_op jit(solution)/shard_map/dot_general | solution.py:65
  159.3 0.3 reduce-scatter.8.cloned.1.call-start
  159.7 0.9 select_n.30
  160.6 2.5 slice_reduce_fusion.14
  163.1 23.5 %reduce-scatter.6.cloned.1.call-done = bf16[384,512]{1,0:T(8,128)(2,1)} async-done(((bf16[384,2048]{1,0:T(8,128)(2,1)}), bf16[384,512]{1,0:T(8,128)(2,1)}) %reduce-scatter.6.cloned.1.call-update) | async-done | bytes 393232 | tf_op jit(solution)/shard_map/reduce_scatter | solution.py:67
  186.6 1.0 broadcast_maximum_fusion
  187.7 4.7 %convolution_divide_fusion = f32[2048,256]{1,0:T(8,128)} fusion(s32[2048]{0:T(1024)S(1)} %get-tuple-element.16, s32[2048]{0:T(1024)S(1)} %get-tuple-element.17, s32[2048]{0:T(1024)S(1)} %get-tuple-element.18, s32[2048]{0:T(1024)S(1)} %get-tuple-element.19, s32[2048]{0:T(1024)S(1)} %get-tuple-element.15, bf16[512,256]{1,0:T(8,128)(2,1)S(1)} %copy-done.4, ...), kind=kOutput, calls=%fused_computation.30 | convolution fusion | flops 515932160 | bytes 2801664 | tf_op jit(solution)/shard_map/dot_general | solution.py:74
  192.4 1.9 fusion.17
  194.2 138.1 %reduce-scatter.8.cloned.1.call-done = f32[64,256]{1,0:T(8,128)} async-done(((f32[2048,256]{1,0:T(8,128)}), f32[64,256]{1,0:T(8,128)}) %reduce-scatter.8.cloned.1.call-update) | async-done | bytes 65552 | tf_op jit(solution)/shard_map/reduce_scatter | solution.py:79
  332.4 0.9 multiply_reduce_fusion
  333.3 1.5 multiply_convert_fusion
  (29 shorter events, 0.9 us)
Async XLA Ops:
  6.5 73.2 %copy-start = (bf16[512,2048]{1,0:T(8,128)(2,1)S(1)}, bf16[512,2048]{1,0:T(8,128)(2,1)}, u32[]{:S(2)}) copy-start(bf16[512,2048]{1,0:T(8,128)(2,1)} %param.12) | copy-start | bytes 6291460
  6.5 148.0 %reduce-scatter.4.cloned.1.call-start = ((), (), s32[]{:S(2)}) async-start(), calls=%async_computation.3 | async-start | bytes 3538944 | tf_op jit(solution)/shard_map/reduce_scatter | solution.py:59
  51.7 7.9 %copy-start.2 = (bf16[1024,512]{1,0:T(8,128)(2,1)S(1)}, bf16[1024,512]{1,0:T(8,128)(2,1)}, u32[]{:S(2)}) copy-start(bf16[1024,512]{1,0:T(8,128)(2,1)} %param.10) | copy-start | bytes 3145732
  51.7 7.9 %copy-start.5 = (bf16[4,512]{1,0:T(4,128)(2,1)S(1)}, bf16[4,512]{1,0:T(4,128)(2,1)}, u32[]{:S(2)}) copy-start(bf16[4,512]{1,0:T(4,128)(2,1)} %param.11) | copy-start | bytes 12292
  79.1 0.7 copy-start.3
  79.1 107.5 %reduce-scatter.6.cloned.1.call-start = ((), (), s32[]{:S(2)}) async-start(), calls=%async_computation.4 | async-start | bytes 1966080 | tf_op jit(solution)/shard_map/reduce_scatter | solution.py:67
  159.3 173.0 %reduce-scatter.8.cloned.1.call-start = ((), (), s32[]{:S(2)}) async-start(), calls=%async_computation.5 | async-start | bytes 2162688 | tf_op jit(solution)/shard_map/reduce_scatter | solution.py:79
  160.6 27.1 %copy-start.4 = (bf16[512,256]{1,0:T(8,128)(2,1)S(1)}, bf16[512,256]{1,0:T(8,128)(2,1)}, u32[]{:S(2)}) copy-start(bf16[512,256]{1,0:T(8,128)(2,1)} %param.15) | copy-start | bytes 786436
  187.6 4.7 %copy-start.1 = (bf16[512,256]{1,0:T(8,128)(2,1)S(1)}, bf16[512,256]{1,0:T(8,128)(2,1)}, u32[]{:S(2)}) copy-start(bf16[512,256]{1,0:T(8,128)(2,1)} %param.14) | copy-start | bytes 786436
Sparse Core Ops, SparseCore 0:
  79.2 75.2 reduce-scatter.3
  159.5 27.0 reduce-scatter.5
  194.4 137.9 reduce-scatter.7

commit v2 on v1

v2 whole, which is shorter than its diff:
```python
import functools

import jax
import jax.numpy as jnp
from jax import lax
from jax.experimental import pallas as pl
from jax.experimental.pallas import tpu as pltpu
from jax.sharding import PartitionSpec as P

MESH = pl.DeviceIdType.MESH
CORES = 2


def greet(peers):
    barrier = pltpu.get_barrier_semaphore()
    for peer in peers:
        pl.semaphore_signal(barrier, inc=1, device_id=peer, device_id_type=MESH)
    pl.semaphore_wait(barrier, len(peers))


def remote(src, dst, sends, recvs, peer):
    return pltpu.make_async_remote_copy(
        src_ref=src, dst_ref=dst, send_sem=sends, recv_sem=recvs, device_id=peer, device_id_type=MESH
    )


def gather_kernel(shards, own_ref, all_ref, sends, recvs, here):
    me = lax.axis_index("node")
    peers = [{"node": lax.rem(me + off, shards)} for off in range(1, shards)]
    greet(peers)
    copies = []
    for at, peer in enumerate(peers):
        copy = remote(own_ref, all_ref.at[me], sends.at[at], recvs.at[at], peer)
        copy.start()
        copies.append(copy)
    local = pltpu.make_async_copy(own_ref, all_ref.at[me], here)
    local.start()
    local.wait()
    for copy in copies:
        copy.wait()


def gather_lists(packed, shards):
    return pl.pallas_call(
        functools.partial(gather_kernel, shards),
        out_shape=jax.ShapeDtypeStruct((shards,) + packed.shape, packed.dtype),
        in_specs=[pl.BlockSpec(memory_space=pltpu.VMEM)],
        out_specs=pl.BlockSpec(memory_space=pltpu.VMEM),
        scratch_shapes=[
            pltpu.SemaphoreType.DMA((shards - 1,)),
            pltpu.SemaphoreType.DMA((shards - 1,)),
            pltpu.SemaphoreType.DMA,
        ],
        compiler_params=pltpu.CompilerParams(collective_id=0, has_side_effects=True),
    )(packed)


def count_tiles(local, fan, width, out_ref, row0):
    rows = local.shape[0]
    for start in range(0, width, 128):
        columns = lax.broadcasted_iota(jnp.int32, (rows, 128), 1) + start
        total = jnp.zeros((rows, 128), jnp.float32)
        for k in range(fan):
            total = total + jnp.where(local[:, k : k + 1] == columns, 1.0, 0.0)
        out_ref[pl.ds(row0, rows), start : start + 128] = total.astype(jnp.bfloat16)


def main_kernel(
    sizes,
    table_ref,
    hub_ref,
    self_one,
    pool_one,
    self_two,
    pool_two,
    local_one,
    local_two,
    counts_ref,
    out_ref,
    matrix,
    matrix_two,
    hubs,
    acc,
    x_send,
    x_recv,
    z_send,
    z_recv,
    part,
    c_send,
    c_recv,
    y_send,
    y_recv,
    mixed,
    mc_recv,
    my_send,
    my_recv,
    mx_send,
    mx_recv,
    mz_send,
    mz_recv,
    x_ss,
    x_rs,
    z_ss,
    z_rs,
    c_ss,
    c_rs,
    y_ss,
    y_rs,
    mc_ss,
    mc_rs,
    my_ss,
    my_rs,
    mx_ss,
    mx_rs,
    mz_ss,
    mz_rs,
):
    big_z, big_x, big_y, fan_one, fan_two = sizes
    f32, bf16 = jnp.float32, jnp.bfloat16
    node = lax.axis_index("node")
    feat = lax.axis_index("feat")
    z, x = node // big_x, lax.rem(node, big_x)
    y, core = feat // CORES, lax.rem(feat, CORES)
    x_peers = [{"node": z * big_x + lax.rem(x + o, big_x)} for o in range(1, big_x)]
    z_peers = [{"node": lax.rem(z + o, big_z) * big_x + x} for o in range(1, big_z)]
    y_peers = [{"feat": lax.rem(y + o, big_y) * CORES + core} for o in range(1, big_y)]
    other = 1 - core
    c_peer = {"feat": y * CORES + other}
    greet(x_peers + z_peers + y_peers + [c_peer])

    rows, width = table_ref.shape
    front = acc.shape[0]
    reach = matrix.shape[1]
    hubs[...] = jnp.zeros_like(hubs)
    hubs[0 : hub_ref.shape[0], :] = hub_ref[...]

    def sums_for(target):
        def fill(at, carry):
            row0 = pl.multiple_of(at * 32, 32)
            local = local_one[pl.ds(pl.multiple_of(target * front + row0, 32), 32), :]
            count_tiles(local, fan_one, reach, matrix, row0)
            return carry

        lax.fori_loop(0, front // 32, fill, 0)
        return jnp.dot(
            matrix[:, 0:rows], table_ref[...], preferred_element_type=f32
        ) + jnp.dot(matrix[:, rows:reach], hubs[...], preferred_element_type=f32)

    def x_copy(s, o):
        return remote(
            x_send.at[s, o], x_recv.at[s, o], x_ss.at[s, o], x_rs.at[s, o], x_peers[o]
        )

    def first_phase(s, carry):
        zt = lax.rem(z + 1 + s, big_z)
        for o in range(big_x - 1):
            x_send[s, o] = sums_for(zt * big_x + lax.rem(x + 1 + o, big_x)).astype(bf16)
            x_copy(s, o).start()
        return carry

    lax.fori_loop(0, big_z, first_phase, 0)

    def z_copy(s, to):
        peer = {"node": to * big_x + x}
        return remote(z_send.at[s], z_recv.at[s], z_ss.at[s], z_rs.at[s], peer)

    def second_phase(s, carry):
        zt = lax.rem(z + 1 + s, big_z)
        acc[...] = sums_for(zt * big_x + x)
        for o in range(big_x - 1):
            x_copy(s, o).wait()
            acc[...] += x_recv[s, o].astype(f32)

        @pl.when(s < big_z - 1)
        def _():
            z_send[s] = acc[...].astype(bf16)
            z_copy(s, zt).start()

        return carry

    lax.fori_loop(0, big_z, second_phase, 0)

    hidden_part = part.shape[2]
    feats = big_y * CORES

    def own_part(f, carry):
        at = pl.ds(pl.multiple_of(f * hidden_part, 128), hidden_part)
        part[f] = jnp.dot(table_ref[0:front, :], self_one[:, at], preferred_element_type=f32)
        return carry

    lax.fori_loop(0, feats, own_part, 0)
    targets = matrix_two.shape[0]

    def fill_two(at, carry):
        row0 = pl.multiple_of(at * 32, 32)
        count_tiles(local_two[pl.ds(row0, 32), :], fan_two, front, matrix_two, row0)
        return carry

    lax.fori_loop(0, targets // 32, fill_two, 0)

    for s in range(big_z - 1):
        z_copy(s, lax.rem(z + 1 + s, big_z)).wait()
        acc[...] += z_recv[s].astype(f32)
    mean = (acc[...] / counts_ref[...].astype(f32)).astype(bf16)
    matrix[:, 0:width] = mean

    def part_of(f):
        at = pl.ds(pl.multiple_of(f * hidden_part, 128), hidden_part)
        return part[f] + jnp.dot(matrix[:, 0:width], pool_one[:, at], preferred_element_type=f32)

    def c_copy(s):
        return remote(c_send.at[s], c_recv.at[s], c_ss.at[s], c_rs.at[s], c_peer)

    def c_phase(s, carry):
        yt = lax.rem(y + 1 + s, big_y)
        c_send[s] = part_of(yt * CORES + other)
        c_copy(s).start()
        return carry

    lax.fori_loop(0, big_y, c_phase, 0)

    def y_copy(s, to):
        peer = {"feat": to * CORES + core}
        return remote(y_send.at[s], y_recv.at[s], y_ss.at[s], y_rs.at[s], peer)

    def y_step(s, carry):
        yt = lax.rem(y + 1 + s, big_y)
        total = part_of(yt * CORES + core)
        c_copy(s).wait()
        total = total + c_recv[s]

        @pl.when(s < big_y - 1)
        def _():
            y_send[s] = total.astype(bf16)
            y_copy(s, yt).start()

        @pl.when(s == big_y - 1)
        def _():
            c_send[s] = total

        return carry

    lax.fori_loop(0, big_y, y_step, 0)
    total = c_send[big_y - 1]
    for s in range(big_y - 1):
        y_copy(s, lax.rem(y + 1 + s, big_y)).wait()
        total = total + y_recv[s].astype(f32)
    hidden = jnp.maximum(total, 0.0).astype(bf16)

    projected = jnp.dot(hidden, pool_two[...], preferred_element_type=f32).astype(bf16)
    piece = out_ref.shape[0]
    own = jnp.dot(hidden[0 : piece * feats], self_two[...], preferred_element_type=f32)
    quarter = big_x * big_z * piece
    for c in range(CORES):
        for yy in range(big_y):
            at = (c * big_y + yy) * quarter
            weight = 1.0 / local_two[at : at + quarter, fan_two : fan_two + 1].astype(f32)
            mixed[c, yy] = (
                jnp.dot(matrix_two[at : at + quarter, :], projected, preferred_element_type=f32)
                * weight
            )
            row = pl.multiple_of((x * big_z + z) * piece, 8)
            f = yy * CORES + c
            mixed[c, yy, pl.ds(row, piece), :] += own[f * piece : (f + 1) * piece]

    mc = remote(mixed.at[other], mc_recv, mc_ss, mc_rs, c_peer)
    mc.start()
    mc.wait()
    y_copies = []
    for o in range(big_y - 1):
        yt = lax.rem(y + 1 + o, big_y)
        my_send[o] = (mixed[core, yt] + mc_recv[yt]).astype(bf16)
        copy = remote(my_send.at[o], my_recv.at[o], my_ss.at[o], my_rs.at[o], y_peers[o])
        copy.start()
        y_copies.append(copy)
    total = mixed[core, y] + mc_recv[y]
    for o, copy in enumerate(y_copies):
        copy.wait()
        total = total + my_recv[o].astype(f32)
    mixed[core, y] = total
    slab = big_z * piece
    x_copies = []
    for o in range(big_x - 1):
        row = pl.multiple_of(lax.rem(x + 1 + o, big_x) * slab, 8)
        mx_send[o] = mixed[core, y, pl.ds(row, slab), :].astype(bf16)
        copy = remote(mx_send.at[o], mx_recv.at[o], mx_ss.at[o], mx_rs.at[o], x_peers[o])
        copy.start()
        x_copies.append(copy)
    total = mixed[core, y, pl.ds(pl.multiple_of(x * slab, 8), slab), :]
    for o, copy in enumerate(x_copies):
        copy.wait()
        total = total + mx_recv[o].astype(f32)
    mz_send[...] = total
    z_copies = []
    for o in range(big_z - 1):
        row = pl.multiple_of(lax.rem(z + 1 + o, big_z) * piece, 8)
        copy = remote(
            mz_send.at[pl.ds(row, piece)], mz_recv.at[o], mz_ss.at[o], mz_rs.at[o], z_peers[o]
        )
        copy.start()
        z_copies.append(copy)
    total = mz_send[pl.ds(pl.multiple_of(z * piece, 8), piece), :]
    for o, copy in enumerate(z_copies):
        copy.wait()
        total = total + mz_recv[o]
    scale = lax.rsqrt(jnp.mean(total * total, axis=1, keepdims=True) + 1e-06)
    out_ref[...] = (total * scale).astype(bf16)


def body(
    feature_table,
    hub_table,
    first_self,
    first_pooled,
    second_self,
    second_pooled,
    first_lists,
    first_counts,
    second_lists,
    second_counts,
):
    shards = lax.axis_size("node")
    feats = lax.axis_size("feat")
    big_x = 2 ** ((shards.bit_length() - 1) // 2)
    big_z = shards // big_x
    big_y = feats // CORES
    me = lax.axis_index("node")
    rows_here, width = feature_table.shape
    hubs_here = hub_table.shape[0]
    front, fan_one = first_lists.shape
    targets_here, fan_two = second_lists.shape
    total_rows = rows_here * shards
    piece = targets_here // feats
    out_width = second_self.shape[1]
    hidden_part = second_self.shape[0]

    slots_one = jnp.arange(fan_one, dtype=jnp.int32)[None, :]
    slots_two = jnp.arange(fan_two, dtype=jnp.int32)[None, :]
    lists_one = jnp.where(slots_one < first_counts[:, None], first_lists, -1).T
    lists_two = jnp.where(slots_two < second_counts[:, None], second_lists, -1).T
    lists_two = jnp.concatenate([lists_two, second_counts[None, :]], axis=0)
    lists_two = jnp.pad(lists_two, ((0, 0), (0, front - targets_here)))
    packed = jnp.concatenate([lists_one, lists_two], axis=0)
    everyone = gather_lists(packed, shards)
    all_one = everyone[:, :fan_one].transpose(0, 2, 1).reshape(shards * front, fan_one)
    all_two = everyone[:, fan_one:, :targets_here]

    feature_at = all_one - me * rows_here
    hub_at = all_one - total_rows - me * hubs_here
    local_one = jnp.where(
        (feature_at >= 0) & (feature_at < rows_here) & (all_one >= 0),
        feature_at,
        jnp.where((hub_at >= 0) & (hub_at < hubs_here), hub_at + rows_here, -1),
    )
    is_count = (jnp.arange(fan_two + 1) == fan_two)[None, :, None]
    local_two = jnp.where(
        is_count, all_two, jnp.where(all_two >= 0, all_two - me * front, -1)
    )
    local_two = local_two.reshape(big_z, big_x, fan_two + 1, big_y, CORES, piece)
    local_two = local_two.transpose(4, 3, 1, 0, 5, 2).reshape(-1, fan_two + 1)

    reach = rows_here + 128
    bf16, f32 = jnp.bfloat16, jnp.float32
    dma = pltpu.SemaphoreType.DMA
    zs, xs, ys = big_z - 1, big_x - 1, big_y - 1
    quarter = big_x * big_z * piece
    slab = big_z * piece
    block = (front, width)
    hblock = (front, hidden_part)
    vmem = pl.BlockSpec(memory_space=pltpu.VMEM)
    return pl.pallas_call(
        functools.partial(main_kernel, (big_z, big_x, big_y, fan_one, fan_two)),
        out_shape=jax.ShapeDtypeStruct((piece, out_width), bf16),
        in_specs=[vmem] * 9,
        out_specs=vmem,
        scratch_shapes=[
            pltpu.VMEM((front, reach), bf16),
            pltpu.VMEM((targets_here * shards, front), bf16),
            pltpu.VMEM((128, width), bf16),
            pltpu.VMEM(block, f32),
            pltpu.VMEM((big_z, xs) + block, bf16),
            pltpu.VMEM((big_z, xs) + block, bf16),
            pltpu.VMEM((zs,) + block, bf16),
            pltpu.VMEM((zs,) + block, bf16),
            pltpu.VMEM((feats,) + hblock, f32),
            pltpu.VMEM((big_y,) + hblock, f32),
            pltpu.VMEM((big_y,) + hblock, f32),
            pltpu.VMEM((ys,) + hblock, bf16),
            pltpu.VMEM((ys,) + hblock, bf16),
            pltpu.VMEM((CORES, big_y, quarter, out_width), f32),
            pltpu.VMEM((big_y, quarter, out_width), f32),
            pltpu.VMEM((ys, quarter, out_width), bf16),
            pltpu.VMEM((ys, quarter, out_width), bf16),
            pltpu.VMEM((xs, slab, out_width), bf16),
            pltpu.VMEM((xs, slab, out_width), bf16),
            pltpu.VMEM((slab, out_width), f32),
            pltpu.VMEM((zs, piece, out_width), f32),
            dma((big_z, xs)),
            dma((big_z, xs)),
            dma((zs,)),
            dma((zs,)),
            dma((big_y,)),
            dma((big_y,)),
            dma((ys,)),
            dma((ys,)),
            dma,
            dma,
            dma((ys,)),
            dma((ys,)),
            dma((xs,)),
            dma((xs,)),
            dma((zs,)),
            dma((zs,)),
        ],
        compiler_params=pltpu.CompilerParams(
            collective_id=1, has_side_effects=True, vmem_limit_bytes=60 * 1024 * 1024
        ),
    )(
        feature_table,
        hub_table,
        first_self,
        first_pooled,
        second_self,
        second_pooled,
        local_one,
        local_two,
        first_counts[:, None],
    )


def solution(mesh):
    return jax.shard_map(
        body,
        mesh=mesh,
        in_specs=(
            P("node", "feat"),
            P("node", "feat"),
            P("feat", None),
            P("feat", None),
            P("feat", None),
            P("feat", None),
            P("node", None),
            P("node"),
            P("node", None),
            P("node"),
        ),
        out_specs=P(("node", "feat"), None),
        check_vma=False,
    )
```

time: 342 us -> 119 us (0.35)
  waiting for transfers between devices: 233 us -> 0 us
  Pallas kernels: 0 us -> 106 us
  matrix products: 34.4 us -> 0 us
  blocking collectives: 32.4 us -> 0 us
  local copies, waits for them, and re-layouts: 20 us -> 5.99 us
  between operations: 13.3 us -> 0.08 us
    reduce_scatter x3 -> x0, waiting for transfers between devices: 233 us -> none  [the longest x1 138 us: body(): lax.psum_scatter(mixed, ('node', 'feat'), scatter_dimension=0, tiled=True)]
    pallas_call x0 -> x2, Pallas kernels: none -> 106 us  [the longest x1 94.6 us: body(): pl.pallas_call(functools.partial(main_kernel, (big_z, big_x, big_y, fan_o...]
    dot_general x5 -> x0, matrix products: 34.4 us -> none  [the longest x1 19.4 us: body(): sums = jnp.dot(matrix_one, combined, preferred_element_type=jnp.float32)]
    all_gather x1 -> x0, blocking collectives: 32.4 us -> none  [body(): everyone = lax.all_gather(packed, 'node', axis=0, tiled=True)]
    slice x2 -> x0, local copies, waits for them, and re-layouts: 10.4 us -> none  [count_matrix(): total = total + (local[:, k:k + 1] == columns).astype(jnp.float32)]
  transfers between devices with their start and end apart: 3 -> 0, of which waited for: 3 -> 0; matrix products, arithmetic and copies ran while one was open for 2% -> 0% of each run, Pallas kernels for 0% -> 0%
where the time goes in v2:
time: 119 us
  Pallas kernels  106 us (89%)
  other arithmetic  6.63 us (6%)
  local copies, waits for them, and re-layouts  5.99 us (5%)
    pallas_call x1, Pallas kernels, body(): pl.pallas_call(functools.partial(main_kernel, (big_z, big_x, big_y, fan_o...  94.6 us
    pallas_call x1, Pallas kernels, gather_lists(): pl.pallas_call(functools.partial(gather_kernel, shards), out_shape=jax.Sh...  11.2 us
    select_n x1, other arithmetic, body(): jnp.where((feature_at >= 0) & (feature_at < rows_here) & (all_one >= 0),...  2.78 us

profile of v2, /device:TPU:0, one launch (start us, length us, event | category | flops | bytes accessed | tf_op | source)
XLA Modules:
  0.0 118.6 jit_solution(7940353096516582713)
XLA Ops:
  0.0 0.7 select_bitcast_fusion.1
  0.7 0.7 select_bitcast_fusion.2
  1.4 0.7 pad_add_fusion.1
  2.1 0.6 pad_add_fusion.own_ref
  2.8 11.2 %shard_map.100 = s32[8,16,384]{2,1,0:T(8,128)} custom-call(s32[16,384]{1,0:T(8,128)} %pad_add_fusion.own_ref), custom_call_target="tpu_custom_call" | custom-call | tf_op jit(solution)/shard_map/pallas_call | solution.py:44
  14.0 1.0 subtract_bitcast_fusion
  15.0 0.0 copy-start
  15.0 0.5 copy.15
  15.5 0.5 copy.17
  16.0 0.0 copy-done
  16.1 1.3 %copy.16 = pred[8,384,10]{2,1,0:T(8,128)(4,1)} copy(pred[8,384,10]{1,2,0:T(8,128)(4,1)S(1)} %compare_bitcast_fusion) | data formatting | bytes 61440 | tf_op jit(solution)/shard_map/ge | solution.py:351
  17.4 0.0 copy-start.1
  17.4 2.8 %bitcast_select_fusion.local_one = s32[3072,10]{1,0:T(8,128)} fusion(s32[8,384,10]{2,1,0:T(8,128)S(1)} %copy.17, s32[8,384,10]{2,1,0:T(8,128)S(1)} %copy.15, pred[8,384,10]{2,1,0:T(8,128)(4,1)} %copy.16), kind=kLoop, calls=%fused_computation | loop fusion | flops 153600 | bytes 399360 | tf_op jit(solution)/shard_map/jit(_where)/select_n | solution.py:350
  20.2 0.1 select_select_fusion
  20.3 0.1 reshape.28
  20.4 1.4 %copy.19 = s32[2,2,2,4,64,6]{5,4,3,2,1,0:T(8,128)} copy(s32[2,2,2,4,64,6]{4,0,1,2,3,5:T(2,128)S(1)} %bitcast.32) | data formatting | bytes 98304 | tf_op jit(solution)/shard_map/transpose | solution.py:360
  21.8 0.0 copy-done.1
  21.8 0.8 broadcast_in_dim.42.counts_ref
  22.6 94.6 %shard_map.101 = bf16[64,256]{1,0:T(8,128)(2,1)} custom-call(bf16[1024,512]{1,0:T(8,128)(2,1)} %table_ref.1, bf16[4,512]{1,0:T(4,128)(2,1)} %hub_ref.1, bf16[512,2048]{1,0:T(8,128)(2,1)} %self_one.1, bf16[512,2048]{1,0:T(8,128)(2,1)} %pool_one.1, bf16[512,256]{1,0:T(8,128)(2,1)} %self_two.1, bf16[512,256]{1,0:T(8,128)(2,1)} %pool_two.1, ...), custom_call_target="tpu_custom_call" | custom-call | tf_op jit(solution)/shard_map/pallas_call | solution.py:371
  117.2 1.4 %copy.22 = bf16[64,256]{1,0:T(8,128)(2,1)} copy(bf16[64,256]{1,0:T(8,128)(2,1)} %shard_map.101) | data formatting | bytes 65536
  (3 shorter events, 0.1 us)
Async XLA Ops:
  15.0 1.0 copy-start
  17.4 4.4 %copy-start.1 = (s32[384]{0:T(512)S(1)}, s32[384]{0:T(512)}, u32[]{:S(2)}) copy-start(s32[384]{0:T(512)} %param.17) | copy-start | bytes 4612

commit v3 on v2

v3 whole, which is shorter than its diff:
```python
import functools

import jax
import jax.numpy as jnp
from jax import lax
from jax.experimental import pallas as pl
from jax.experimental.pallas import tpu as pltpu
from jax.sharding import PartitionSpec as P

MESH = pl.DeviceIdType.MESH
CORES = 2


def greet(peers):
    barrier = pltpu.get_barrier_semaphore()
    for peer in peers:
        pl.semaphore_signal(barrier, inc=1, device_id=peer, device_id_type=MESH)
    pl.semaphore_wait(barrier, len(peers))


def remote(src, dst, sends, recvs, peer):
    return pltpu.make_async_remote_copy(
        src_ref=src, dst_ref=dst, send_sem=sends, recv_sem=recvs, device_id=peer, device_id_type=MESH
    )


def count_tiles(local, fan, width, store):
    rows = local.shape[0]
    local = local.astype(jnp.int16)
    one, zero = jnp.bfloat16(1), jnp.bfloat16(0)
    for start in range(0, width, 128):
        columns = (lax.broadcasted_iota(jnp.int32, (rows, 128), 1) + start).astype(jnp.int16)
        total = jnp.zeros((rows, 128), jnp.bfloat16)
        for k in range(fan):
            picked = jnp.broadcast_to(local[:, k : k + 1], (rows, 128))
            total = total + jnp.where(picked == columns, one, zero)
        store(start, total)


def main_kernel(
    sizes,
    table_ref,
    hub_ref,
    self_one,
    pool_one,
    self_two,
    pool_two,
    packed_ref,
    counts_ref,
    out_ref,
    lists,
    local,
    tables,
    matrix,
    matrix_two,
    weights,
    means,
    acc,
    z_send,
    z_recv,
    part,
    c_send,
    c_recv,
    y_send,
    y_recv,
    mixed,
    mc_recv,
    my_send,
    my_recv,
    mx_send,
    mx_recv,
    acc_z,
    mz_send,
    mz_recv,
    n_ss,
    n_rs,
    x_ss,
    x_rs,
    h_ss,
    h_rs,
    z_ss,
    z_rs,
    c_ss,
    c_rs,
    y_ss,
    y_rs,
    mc_ss,
    mc_rs,
    my_ss,
    my_rs,
    mx_ss,
    mx_rs,
    mz_ss,
    mz_rs,
):
    big_z, big_x, big_y, fan_one, fan_two, hubs_here, halves = sizes
    f32, bf16 = jnp.float32, jnp.bfloat16
    node = lax.axis_index("node")
    feat = lax.axis_index("feat")
    z, x = node // big_x, lax.rem(node, big_x)
    y, core = feat // CORES, lax.rem(feat, CORES)
    x_peers = [{"node": z * big_x + lax.rem(x + o, big_x)} for o in range(1, big_x)]
    z_peers = [{"node": lax.rem(z + o, big_z) * big_x + x} for o in range(1, big_z)]
    y_peers = [{"feat": lax.rem(y + o, big_y) * CORES + core} for o in range(1, big_y)]
    other = 1 - core
    c_peer = {"feat": y * CORES + other}
    shards = big_z * big_x
    n_peers = [{"node": lax.rem(node + o, shards)} for o in range(1, shards)]
    greet(n_peers + y_peers + [c_peer])

    rows, width = table_ref.shape
    front = acc.shape[0]
    reach = tables.shape[1]
    part_width = width // halves

    list_copies = []
    for o, peer in enumerate(n_peers):
        copy = remote(packed_ref, lists.at[node], n_ss.at[o], n_rs.at[o], peer)
        copy.start()
        list_copies.append(copy)
    table_copies = []
    for h in range(halves):
        cut = pl.ds(h * part_width, part_width)
        for o, peer in enumerate(x_peers):
            copy = remote(
                table_ref.at[:, cut],
                tables.at[1 + o, pl.ds(0, rows), cut],
                x_ss.at[h, o],
                x_rs.at[h, o],
                peer,
            )
            copy.start()
            table_copies.append(copy)
        if h == 0:
            for o, peer in enumerate(x_peers):
                copy = remote(
                    hub_ref,
                    tables.at[1 + o, pl.ds(rows, hub_ref.shape[0])],
                    h_ss.at[o],
                    h_rs.at[o],
                    peer,
                )
                copy.start()
                table_copies.append(copy)
    first_copies = 2 * len(x_peers)
    lists[node] = packed_ref[...]
    tail = rows + hub_ref.shape[0]
    tables[0, 0:rows] = table_ref[...]
    tables[0, rows:tail] = hub_ref[...]
    for slot in range(big_x):
        tables[slot, tail:reach] = jnp.zeros((reach - tail, width), bf16)
    for copy in list_copies:
        copy.wait()

    def decode(n, carry):
        entry = lists[n]
        found = jnp.full(entry.shape, -1, jnp.int32)
        for slot in range(big_x):
            owner = z * big_x + lax.rem(x - slot + big_x, big_x)
            feature_at = entry - owner * rows
            hub_at = entry - shards * rows - owner * hubs_here
            found = jnp.where(
                (feature_at >= 0) & (feature_at < rows), feature_at + slot * reach, found
            )
            found = jnp.where(
                (hub_at >= 0) & (hub_at < hubs_here), hub_at + (slot * reach + rows), found
            )
        line = lax.broadcasted_iota(jnp.int32, entry.shape, 0)
        seconds = jnp.clip(entry - node * front, -1, front)
        seconds = jnp.where(line == fan_one + fan_two, entry, seconds)
        local[n] = jnp.where(line < fan_one, found, seconds).T
        return carry

    lax.fori_loop(0, shards, decode, 0)

    def fill(target, at):
        def step(i, carry):
            row0 = pl.multiple_of(i * 32, 32)

            def store(start, value):
                matrix[at, pl.ds(row0, 32), start : start + 128] = value

            count_tiles(local[target, pl.ds(row0, 32), :], fan_one, reach * big_x, store)
            return carry

        lax.fori_loop(0, front // 32, step, 0)

    def sums_of(at, low, high):
        total = jnp.dot(matrix[at, :, 0:reach], tables[0, :, low:high], preferred_element_type=f32)
        for slot in range(1, big_x):
            total = total + jnp.dot(
                matrix[at, :, slot * reach : (slot + 1) * reach],
                tables[slot, :, low:high],
                preferred_element_type=f32,
            )
        return total

    def z_copy(h, s, to):
        peer = {"node": to * big_x + x}
        return remote(z_send.at[h, s], z_recv.at[h, s], z_ss.at[h, s], z_rs.at[h, s], peer)

    slots = matrix.shape[0]
    fill(lax.rem(z + 1, big_z) * big_x + x, 0)
    for copy in table_copies[:first_copies]:
        copy.wait()

    def first_half(s, carry):
        zt = lax.rem(z + 1 + s, big_z)
        at = lax.rem(s, slots)

        @pl.when(s > 0)
        def _():
            fill(zt * big_x + x, at)

        z_send[0, s] = sums_of(at, 0, part_width).astype(bf16)
        z_copy(0, s, zt).start()
        return carry

    lax.fori_loop(0, big_z - 1, first_half, 0)
    for copy in table_copies[first_copies:]:
        copy.wait()
    for h in range(1, halves):

        def other_half(s, carry, h=h):
            z_send[h, s] = sums_of(s, h * part_width, (h + 1) * part_width).astype(bf16)
            z_copy(h, s, lax.rem(z + 1 + s, big_z)).start()
            return carry

        lax.fori_loop(0, big_z - 1, other_half, 0)
    fill(node, 0)
    acc[...] = sums_of(0, 0, width)

    hidden_part = part.shape[2]
    feats = big_y * CORES

    def own_part(f, carry):
        at = pl.ds(pl.multiple_of(f * hidden_part, 128), hidden_part)
        part[f] = jnp.dot(table_ref[0:front, :], self_one[:, at], preferred_element_type=f32)
        return carry

    lax.fori_loop(0, feats, own_part, 0)

    piece = out_ref.shape[0]

    def fill_two(at, carry):
        n, f = at // feats, lax.rem(at, feats)
        zz, xx = n // big_x, lax.rem(n, big_x)
        yy, cc = f // CORES, lax.rem(f, CORES)
        to = (((cc * big_y + yy) * big_x + xx) * big_z + zz) * piece
        from_row = pl.multiple_of(f * piece, 16)
        to_row = pl.multiple_of(to, 16)
        block = local[n, pl.ds(from_row, piece), :]

        def store(start, value):
            matrix_two[pl.ds(to_row, piece), start : start + 128] = value

        count_tiles(block[:, fan_one : fan_one + fan_two], fan_two, front, store)
        weights[pl.ds(to_row, piece), :] = 1.0 / block[
            :, fan_one + fan_two : fan_one + fan_two + 1
        ].astype(f32)
        return carry

    lax.fori_loop(0, shards * feats, fill_two, 0)

    for h in range(halves):
        for s in range(big_z - 1):
            z_copy(h, s, lax.rem(z + 1 + s, big_z)).wait()
            acc[:, h * part_width : (h + 1) * part_width] += z_recv[h, s].astype(f32)
    mean = (acc[...] / counts_ref[...].astype(f32)).astype(bf16)
    means[...] = mean

    def part_of(f):
        at = pl.ds(pl.multiple_of(f * hidden_part, 128), hidden_part)
        return part[f] + jnp.dot(means[...], pool_one[:, at], preferred_element_type=f32)

    def c_copy(s):
        return remote(c_send.at[s], c_recv.at[s], c_ss.at[s], c_rs.at[s], c_peer)

    def c_phase(s, carry):
        yt = lax.rem(y + 1 + s, big_y)
        c_send[s] = part_of(yt * CORES + other)
        c_copy(s).start()
        return carry

    lax.fori_loop(0, big_y, c_phase, 0)

    def y_copy(s, to):
        peer = {"feat": to * CORES + core}
        return remote(y_send.at[s], y_recv.at[s], y_ss.at[s], y_rs.at[s], peer)

    def y_step(s, carry):
        yt = lax.rem(y + 1 + s, big_y)
        total = part_of(yt * CORES + core)
        c_copy(s).wait()
        total = total + c_recv[s]

        @pl.when(s < big_y - 1)
        def _():
            y_send[s] = total.astype(bf16)
            y_copy(s, yt).start()

        @pl.when(s == big_y - 1)
        def _():
            c_send[s] = total

        return carry

    lax.fori_loop(0, big_y, y_step, 0)
    total = c_send[big_y - 1]
    for s in range(big_y - 1):
        y_copy(s, lax.rem(y + 1 + s, big_y)).wait()
        total = total + y_recv[s].astype(f32)
    hidden = jnp.maximum(total, 0.0).astype(bf16)

    projected = jnp.dot(hidden, pool_two[...], preferred_element_type=f32).astype(bf16)
    own = jnp.dot(hidden[0 : piece * feats], self_two[...], preferred_element_type=f32)
    quarter = big_x * big_z * piece
    for c in range(CORES):
        for yy in range(big_y):
            at = (c * big_y + yy) * quarter
            weight = weights[at : at + quarter, :]
            mixed[c, yy] = (
                jnp.dot(matrix_two[at : at + quarter, :], projected, preferred_element_type=f32)
                * weight
            )
            row = pl.multiple_of((x * big_z + z) * piece, 8)
            f = yy * CORES + c
            mixed[c, yy, pl.ds(row, piece), :] += own[f * piece : (f + 1) * piece]

    mc = remote(mixed.at[other], mc_recv, mc_ss, mc_rs, c_peer)
    mc.start()
    mc.wait()
    y_copies = []
    for o in range(big_y - 1):
        yt = lax.rem(y + 1 + o, big_y)
        my_send[o] = (mixed[core, yt] + mc_recv[yt]).astype(bf16)
        copy = remote(my_send.at[o], my_recv.at[o], my_ss.at[o], my_rs.at[o], y_peers[o])
        copy.start()
        y_copies.append(copy)
    total = mixed[core, y] + mc_recv[y]
    for o, copy in enumerate(y_copies):
        copy.wait()
        total = total + my_recv[o].astype(f32)
    mixed[core, y] = total
    slab = big_z * piece
    x_copies = []
    for o in range(big_x - 1):
        row = pl.multiple_of(lax.rem(x + 1 + o, big_x) * slab, 8)
        mx_send[o] = mixed[core, y, pl.ds(row, slab), :].astype(bf16)
        copy = remote(mx_send.at[o], mx_recv.at[o], mx_ss.at[o], mx_rs.at[o], x_peers[o])
        copy.start()
        x_copies.append(copy)
    total = mixed[core, y, pl.ds(pl.multiple_of(x * slab, 8), slab), :]
    for o, copy in enumerate(x_copies):
        copy.wait()
        total = total + mx_recv[o].astype(f32)
    acc_z[...] = total
    mz_send[...] = total.astype(bf16)
    z_copies = []
    for o in range(big_z - 1):
        row = pl.multiple_of(lax.rem(z + 1 + o, big_z) * piece, 16)
        copy = remote(
            mz_send.at[pl.ds(row, piece)], mz_recv.at[o], mz_ss.at[o], mz_rs.at[o], z_peers[o]
        )
        copy.start()
        z_copies.append(copy)
    total = acc_z[pl.ds(pl.multiple_of(z * piece, 8), piece), :]
    for o, copy in enumerate(z_copies):
        copy.wait()
        total = total + mz_recv[o].astype(f32)
    scale = lax.rsqrt(jnp.mean(total * total, axis=1, keepdims=True) + 1e-06)
    out_ref[...] = (total * scale).astype(bf16)


def body(
    feature_table,
    hub_table,
    first_self,
    first_pooled,
    second_self,
    second_pooled,
    first_lists,
    first_counts,
    second_lists,
    second_counts,
):
    shards = lax.axis_size("node")
    feats = lax.axis_size("feat")
    big_x = 2 ** ((shards.bit_length() - 1) // 2)
    big_z = shards // big_x
    big_y = feats // CORES
    rows_here, width = feature_table.shape
    hubs_here = hub_table.shape[0]
    front, fan_one = first_lists.shape
    targets_here, fan_two = second_lists.shape
    piece = targets_here // feats
    out_width = second_self.shape[1]
    hidden_part = second_self.shape[0]

    slots_one = jnp.arange(fan_one, dtype=jnp.int32)[None, :]
    slots_two = jnp.arange(fan_two, dtype=jnp.int32)[None, :]
    lists_one = jnp.where(slots_one < first_counts[:, None], first_lists, -1).T
    lists_two = jnp.where(slots_two < second_counts[:, None], second_lists, -1).T
    lists_two = jnp.concatenate([lists_two, second_counts[None, :]], axis=0)
    lists_two = jnp.pad(lists_two, ((0, 0), (0, front - targets_here)))
    packed = jnp.concatenate([lists_one, lists_two], axis=0)
    hubs = jnp.pad(hub_table, ((0, -hubs_here % 16), (0, 0)))
    reach = rows_here + 128
    halves = 2 if width % 256 == 0 else 1
    bf16, f32 = jnp.bfloat16, jnp.float32
    dma = pltpu.SemaphoreType.DMA
    zs, xs, ys = big_z - 1, big_x - 1, big_y - 1
    quarter = big_x * big_z * piece
    slab = big_z * piece
    block = (front, width)
    hblock = (front, hidden_part)
    vmem = pl.BlockSpec(memory_space=pltpu.VMEM)
    return pl.pallas_call(
        functools.partial(main_kernel, (big_z, big_x, big_y, fan_one, fan_two, hubs_here, halves)),
        out_shape=jax.ShapeDtypeStruct((piece, out_width), bf16),
        in_specs=[vmem] * 8,
        out_specs=vmem,
        scratch_shapes=[
            pltpu.VMEM((shards,) + packed.shape, jnp.int32),
            pltpu.VMEM((shards, front, packed.shape[0]), jnp.int32),
            pltpu.VMEM((big_x, reach, width), bf16),
            pltpu.VMEM((zs if halves > 1 else 1, front, big_x * reach), bf16),
            pltpu.VMEM((targets_here * shards, front), bf16),
            pltpu.VMEM((targets_here * shards, 1), f32),
            pltpu.VMEM(block, bf16),
            pltpu.VMEM(block, f32),
            pltpu.VMEM((halves, zs, front, width // halves), bf16),
            pltpu.VMEM((halves, zs, front, width // halves), bf16),
            pltpu.VMEM((feats,) + hblock, f32),
            pltpu.VMEM((big_y,) + hblock, f32),
            pltpu.VMEM((big_y,) + hblock, f32),
            pltpu.VMEM((ys,) + hblock, bf16),
            pltpu.VMEM((ys,) + hblock, bf16),
            pltpu.VMEM((CORES, big_y, quarter, out_width), f32),
            pltpu.VMEM((big_y, quarter, out_width), f32),
            pltpu.VMEM((ys, quarter, out_width), bf16),
            pltpu.VMEM((ys, quarter, out_width), bf16),
            pltpu.VMEM((xs, slab, out_width), bf16),
            pltpu.VMEM((xs, slab, out_width), bf16),
            pltpu.VMEM((slab, out_width), f32),
            pltpu.VMEM((slab, out_width), bf16),
            pltpu.VMEM((zs, piece, out_width), bf16),
            dma((shards - 1,)),
            dma((shards - 1,)),
            dma((halves, xs)),
            dma((halves, xs)),
            dma((xs,)),
            dma((xs,)),
            dma((halves, zs)),
            dma((halves, zs)),
            dma((big_y,)),
            dma((big_y,)),
            dma((ys,)),
            dma((ys,)),
            dma,
            dma,
            dma((ys,)),
            dma((ys,)),
            dma((xs,)),
            dma((xs,)),
            dma((zs,)),
            dma((zs,)),
        ],
        compiler_params=pltpu.CompilerParams(
            collective_id=1, has_side_effects=True, vmem_limit_bytes=60 * 1024 * 1024
        ),
    )(
        feature_table,
        hubs,
        first_self,
        first_pooled,
        second_self,
        second_pooled,
        packed,
        first_counts[:, None],
    )


def solution(mesh):
    return jax.shard_map(
        body,
        mesh=mesh,
        in_specs=(
            P("node", "feat"),
            P("node", "feat"),
            P("feat", None),
            P("feat", None),
            P("feat", None),
            P("feat", None),
            P("node", None),
            P("node"),
            P("node", None),
            P("node"),
        ),
        out_specs=P(("node", "feat"), None),
        check_vma=False,
    )
```

time: 119 us -> 101 us (0.85)
  Pallas kernels: 106 us -> 93.7 us
  other arithmetic: 6.63 us -> 2.75 us
  local copies, waits for them, and re-layouts: 5.99 us -> 4.14 us
    pallas_call x1 -> x0, Pallas kernels: 11.2 us -> none  [gather_lists(): pl.pallas_call(functools.partial(gather_kernel, shards), out_shape=jax.Sh...]
    select_n x2 -> x0, other arithmetic: 2.86 us -> none  [the longest x1 2.78 us: body(): jnp.where((feature_at >= 0) & (feature_at < rows_here) & (all_one >= 0),...]
    transpose x1 -> x0, local copies, waits for them, and re-layouts: 1.38 us -> none  [body(): local_two = local_two.transpose(4, 3, 1, 0, 5, 2).reshape(-1, fan_two + 1)]
    pad x0 -> x1, local copies, waits for them, and re-layouts: none -> 1.3 us  [body(): hubs = jnp.pad(hub_table, ((0, -hubs_here % 16), (0, 0)))]
    ge x1 -> x0, local copies, waits for them, and re-layouts: 1.29 us -> none  [body(): all_one >= 0]
where the time goes in v3:
time: 101 us
  Pallas kernels  93.7 us (93%)
  local copies, waits for them, and re-layouts  4.14 us (4%)
  other arithmetic  2.75 us (3%)
    pallas_call x1, Pallas kernels, body(): pl.pallas_call(functools.partial(main_kernel, (big_z, big_x, big_y, fan_o...  93.7 us

profile of v3, /device:TPU:0, one launch (start us, length us, event | category | flops | bytes accessed | tf_op | source)
XLA Modules:
  0.0 100.6 jit_solution(11911158941947393847)
XLA Ops:
  0.0 0.7 select_bitcast_fusion.1
  0.7 0.7 pad_add_fusion.1
  1.4 1.3 %pad.8.hub_ref = bf16[16,512]{1,0:T(8,128)(2,1)} pad(bf16[4,512]{1,0:T(4,128)(2,1)} %param.11, bf16[]{:T(256)} %constant.1.clone.1), padding=0_12x0_0 | pad | bytes 20482 | tf_op jit(solution)/shard_map/jit(_pad)/pad | solution.py:407
  2.7 0.7 select_bitcast_fusion
  3.4 0.6 pad_add_fusion.packed_ref
  4.0 1.5 %broadcast_in_dim.22.counts_ref = s32[384,1]{1,0:T(8,128)} reshape(s32[384]{0:T(512)} %param.17) | data formatting | bytes 3072 | tf_op jit(solution)/shard_map/broadcast_in_dim | solution.py:402
  5.5 93.7 %shard_map.100 = bf16[64,256]{1,0:T(8,128)(2,1)} custom-call(bf16[1024,512]{1,0:T(8,128)(2,1)} %table_ref.1, bf16[16,512]{1,0:T(8,128)(2,1)} %pad.8.hub_ref, bf16[512,2048]{1,0:T(8,128)(2,1)} %self_one.1, bf16[512,2048]{1,0:T(8,128)(2,1)} %pool_one.1, bf16[512,256]{1,0:T(8,128)(2,1)} %self_two.1, bf16[512,256]{1,0:T(8,128)(2,1)} %pool_two.1, ...), custom_call_target="tpu_custom_call" | custom-call | tf_op jit(solution)/shard_map/pallas_call | solution.py:418
  99.3 1.4 %copy.13 = bf16[64,256]{1,0:T(8,128)(2,1)} copy(bf16[64,256]{1,0:T(8,128)(2,1)} %shard_map.100) | data formatting | bytes 65536

commit v4 on v3

--- a/solution.py
+++ b/solution.py
@@ -63,7 +63,9 @@
     c_recv,
     y_send,
     y_recv,
+    own_ref,
     mixed,
+    mc_send,
     mc_recv,
     my_send,
     my_recv,
@@ -93,7 +95,7 @@
     mz_ss,
     mz_rs,
 ):
-    big_z, big_x, big_y, fan_one, fan_two, hubs_here, halves = sizes
+    big_z, big_x, big_y, fan_one, fan_two, hubs_here, edges = sizes
     f32, bf16 = jnp.float32, jnp.bfloat16
     node = lax.axis_index("node")
     feat = lax.axis_index("feat")
@@ -111,7 +113,7 @@
     rows, width = table_ref.shape
     front = acc.shape[0]
     reach = tables.shape[1]
-    part_width = width // halves
+    halves = len(edges) - 1
 
     list_copies = []
     for o, peer in enumerate(n_peers):
@@ -120,7 +122,7 @@
         list_copies.append(copy)
     table_copies = []
     for h in range(halves):
-        cut = pl.ds(h * part_width, part_width)
+        cut = pl.ds(edges[h], edges[h + 1] - edges[h])
         for o, peer in enumerate(x_peers):
             copy = remote(
                 table_ref.at[:, cut],
@@ -197,7 +199,10 @@
 
     def z_copy(h, s, to):
         peer = {"node": to * big_x + x}
-        return remote(z_send.at[h, s], z_recv.at[h, s], z_ss.at[h, s], z_rs.at[h, s], peer)
+        cut = pl.ds(edges[h], edges[h + 1] - edges[h])
+        return remote(
+            z_send.at[s, :, cut], z_recv.at[s, :, cut], z_ss.at[h, s], z_rs.at[h, s], peer
+        )
 
     slots = matrix.shape[0]
     fill(lax.rem(z + 1, big_z) * big_x + x, 0)
@@ -212,17 +217,19 @@
         def _():
             fill(zt * big_x + x, at)
 
-        z_send[0, s] = sums_of(at, 0, part_width).astype(bf16)
+        z_send[s, :, 0 : edges[1]] = sums_of(at, 0, edges[1]).astype(bf16)
         z_copy(0, s, zt).start()
         return carry
 
     lax.fori_loop(0, big_z - 1, first_half, 0)
-    for copy in table_copies[first_copies:]:
-        copy.wait()
     for h in range(1, halves):
+        begin = first_copies + (h - 1) * len(x_peers)
+        for copy in table_copies[begin : begin + len(x_peers)]:
+            copy.wait()
 
         def other_half(s, carry, h=h):
-            z_send[h, s] = sums_of(s, h * part_width, (h + 1) * part_width).astype(bf16)
+            low, high = edges[h], edges[h + 1]
+            z_send[s, :, low:high] = sums_of(s, low, high).astype(bf16)
             z_copy(h, s, lax.rem(z + 1 + s, big_z)).start()
             return carry
 
@@ -265,7 +272,8 @@
     for h in range(halves):
         for s in range(big_z - 1):
             z_copy(h, s, lax.rem(z + 1 + s, big_z)).wait()
-            acc[:, h * part_width : (h + 1) * part_width] += z_recv[h, s].astype(f32)
+            low, high = edges[h], edges[h + 1]
+            acc[:, low:high] += z_recv[s, :, low:high].astype(f32)
     mean = (acc[...] / counts_ref[...].astype(f32)).astype(bf16)
     means[...] = mean
 
@@ -313,44 +321,54 @@
     hidden = jnp.maximum(total, 0.0).astype(bf16)
 
     projected = jnp.dot(hidden, pool_two[...], preferred_element_type=f32).astype(bf16)
-    own = jnp.dot(hidden[0 : piece * feats], self_two[...], preferred_element_type=f32)
+    own_ref[...] = jnp.dot(hidden[0 : piece * feats], self_two[...], preferred_element_type=f32)
     quarter = big_x * big_z * piece
-    for c in range(CORES):
-        for yy in range(big_y):
-            at = (c * big_y + yy) * quarter
-            weight = weights[at : at + quarter, :]
-            mixed[c, yy] = (
-                jnp.dot(matrix_two[at : at + quarter, :], projected, preferred_element_type=f32)
-                * weight
-            )
-            row = pl.multiple_of((x * big_z + z) * piece, 8)
-            f = yy * CORES + c
-            mixed[c, yy, pl.ds(row, piece), :] += own[f * piece : (f + 1) * piece]
-
-    mc = remote(mixed.at[other], mc_recv, mc_ss, mc_rs, c_peer)
-    mc.start()
-    mc.wait()
-    y_copies = []
-    for o in range(big_y - 1):
-        yt = lax.rem(y + 1 + o, big_y)
-        my_send[o] = (mixed[core, yt] + mc_recv[yt]).astype(bf16)
-        copy = remote(my_send.at[o], my_recv.at[o], my_ss.at[o], my_rs.at[o], y_peers[o])
+    slab = big_z * piece
+
+    def mix(k, s, c, yy):
+        at = pl.ds(pl.multiple_of((c * big_y + yy) * quarter, 16), quarter)
+        mixed[k, s] = (
+            jnp.dot(matrix_two[at, :], projected, preferred_element_type=f32) * weights[at, :]
+        )
+        row = pl.multiple_of((x * big_z + z) * piece, 16)
+        from_row = pl.multiple_of((yy * CORES + c) * piece, 16)
+        mixed[k, s, pl.ds(row, piece), :] += own_ref[pl.ds(from_row, piece), :]
+
+    core_copies = []
+    for s in range(big_y):
+        mix(0, s, other, lax.rem(y + 1 + s, big_y))
+        mc_send[s] = mixed[0, s].astype(bf16)
+        copy = remote(mc_send.at[s], mc_recv.at[s], mc_ss.at[s], mc_rs.at[s], c_peer)
         copy.start()
-        y_copies.append(copy)
-    total = mixed[core, y] + mc_recv[y]
-    for o, copy in enumerate(y_copies):
-        copy.wait()
-        total = total + my_recv[o].astype(f32)
-    mixed[core, y] = total
-    slab = big_z * piece
+        core_copies.append(copy)
+    for s in range(big_y):
+        mix(1, s, core, lax.rem(y + 1 + s, big_y))
+    x_rows = [
+        pl.ds(pl.multiple_of(lax.rem(x + 1 + o, big_x) * slab, 16), slab) for o in range(big_x)
+    ]
+    y_copies = {}
+    for s in range(big_y):
+        core_copies[s].wait()
+        mixed[1, s] += mc_recv[s].astype(f32)
+        if s < big_y - 1:
+            for o in range(big_x):
+                my_send[s, o] = mixed[1, s, x_rows[o], :].astype(bf16)
+                copy = remote(
+                    my_send.at[s, o], my_recv.at[s, o], my_ss.at[s, o], my_rs.at[s, o], y_peers[s]
+                )
+                copy.start()
+                y_copies[s, o] = copy
     x_copies = []
-    for o in range(big_x - 1):
-        row = pl.multiple_of(lax.rem(x + 1 + o, big_x) * slab, 8)
-        mx_send[o] = mixed[core, y, pl.ds(row, slab), :].astype(bf16)
-        copy = remote(mx_send.at[o], mx_recv.at[o], mx_ss.at[o], mx_rs.at[o], x_peers[o])
-        copy.start()
-        x_copies.append(copy)
-    total = mixed[core, y, pl.ds(pl.multiple_of(x * slab, 8), slab), :]
+    for o in range(big_x):
+        total = mixed[1, big_y - 1, x_rows[o], :]
+        for s in range(big_y - 1):
+            y_copies[s, o].wait()
+            total = total + my_recv[s, o].astype(f32)
+        if o < big_x - 1:
+            mx_send[o] = total.astype(bf16)
+            copy = remote(mx_send.at[o], mx_recv.at[o], mx_ss.at[o], mx_rs.at[o], x_peers[o])
+            copy.start()
+            x_copies.append(copy)
     for o, copy in enumerate(x_copies):
         copy.wait()
         total = total + mx_recv[o].astype(f32)
@@ -406,7 +424,8 @@
     packed = jnp.concatenate([lists_one, lists_two], axis=0)
     hubs = jnp.pad(hub_table, ((0, -hubs_here % 16), (0, 0)))
     reach = rows_here + 128
-    halves = 2 if width % 256 == 0 else 1
+    edges = (0, 128, 256, width) if width > 256 else (0, width)
+    halves = len(edges) - 1
     bf16, f32 = jnp.bfloat16, jnp.float32
     dma = pltpu.SemaphoreType.DMA
     zs, xs, ys = big_z - 1, big_x - 1, big_y - 1
@@ -416,7 +435,7 @@
     hblock = (front, hidden_part)
     vmem = pl.BlockSpec(memory_space=pltpu.VMEM)
     return pl.pallas_call(
-        functools.partial(main_kernel, (big_z, big_x, big_y, fan_one, fan_two, hubs_here, halves)),
+        functools.partial(main_kernel, (big_z, big_x, big_y, fan_one, fan_two, hubs_here, edges)),
         out_shape=jax.ShapeDtypeStruct((piece, out_width), bf16),
         in_specs=[vmem] * 8,
         out_specs=vmem,
@@ -429,17 +448,19 @@
             pltpu.VMEM((targets_here * shards, 1), f32),
             pltpu.VMEM(block, bf16),
             pltpu.VMEM(block, f32),
-            pltpu.VMEM((halves, zs, front, width // halves), bf16),
-            pltpu.VMEM((halves, zs, front, width // halves), bf16),
+            pltpu.VMEM((zs,) + block, bf16),
+            pltpu.VMEM((zs,) + block, bf16),
             pltpu.VMEM((feats,) + hblock, f32),
             pltpu.VMEM((big_y,) + hblock, f32),
             pltpu.VMEM((big_y,) + hblock, f32),
             pltpu.VMEM((ys,) + hblock, bf16),
             pltpu.VMEM((ys,) + hblock, bf16),
+            pltpu.VMEM((targets_here, out_width), f32),
             pltpu.VMEM((CORES, big_y, quarter, out_width), f32),
-            pltpu.VMEM((big_y, quarter, out_width), f32),
-            pltpu.VMEM((ys, quarter, out_width), bf16),
-            pltpu.VMEM((ys, quarter, out_width), bf16),
+            pltpu.VMEM((big_y, quarter, out_width), bf16),
+            pltpu.VMEM((big_y, quarter, out_width), bf16),
+            pltpu.VMEM((ys, big_x, slab, out_width), bf16),
+            pltpu.VMEM((ys, big_x, slab, out_width), bf16),
             pltpu.VMEM((xs, slab, out_width), bf16),
             pltpu.VMEM((xs, slab, out_width), bf16),
             pltpu.VMEM((slab, out_width), f32),
@@ -457,10 +478,10 @@
             dma((big_y,)),
             dma((ys,)),
             dma((ys,)),
-            dma,
-            dma,
-            dma((ys,)),
-            dma((ys,)),
+            dma((big_y,)),
+            dma((big_y,)),
+            dma((ys, big_x)),
+            dma((ys, big_x)),
             dma((xs,)),
             dma((xs,)),
             dma((zs,)),

time: 101 us -> 92.8 us (0.919)
  Pallas kernels: 93.7 us -> 85.6 us
    pallas_call x1, Pallas kernels: 93.7 us -> 85.6 us  [body(): pl.pallas_call(functools.partial(main_kernel, (big_z, big_x, big_y, fan_o...]
where the time goes in v4:
time: 92.8 us; the launch traced here: 92.5 us
  Pallas kernels  85.6 us (92%)
  local copies, waits for them, and re-layouts  4.14 us (4%)
  other arithmetic  2.75 us (3%)
    pallas_call x1, Pallas kernels, body(): pl.pallas_call(functools.partial(main_kernel, (big_z, big_x, big_y, fan_o...  85.6 us

profile of v4, /device:TPU:0, one launch (start us, length us, event | category | flops | bytes accessed | tf_op | source)
XLA Modules:
  0.0 92.5 jit_solution(16718399975359812556)
XLA Ops:
  0.0 0.7 select_bitcast_fusion.1
  0.7 0.7 pad_add_fusion.1
  1.4 1.3 %pad.8.hub_ref = bf16[16,512]{1,0:T(8,128)(2,1)} pad(bf16[4,512]{1,0:T(4,128)(2,1)} %param.11, bf16[]{:T(256)} %constant.1.clone.1), padding=0_12x0_0 | pad | bytes 20482 | tf_op jit(solution)/shard_map/jit(_pad)/pad | solution.py:425
  2.7 0.7 select_bitcast_fusion
  3.4 0.6 pad_add_fusion.packed_ref
  4.0 1.5 %broadcast_in_dim.22.counts_ref = s32[384,1]{1,0:T(8,128)} reshape(s32[384]{0:T(512)} %param.17) | data formatting | bytes 3072 | tf_op jit(solution)/shard_map/broadcast_in_dim | solution.py:420
  5.5 85.6 %shard_map.100 = bf16[64,256]{1,0:T(8,128)(2,1)} custom-call(bf16[1024,512]{1,0:T(8,128)(2,1)} %table_ref.1, bf16[16,512]{1,0:T(8,128)(2,1)} %pad.8.hub_ref, bf16[512,2048]{1,0:T(8,128)(2,1)} %self_one.1, bf16[512,2048]{1,0:T(8,128)(2,1)} %pool_one.1, bf16[512,256]{1,0:T(8,128)(2,1)} %self_two.1, bf16[512,256]{1,0:T(8,128)(2,1)} %pool_two.1, ...), custom_call_target="tpu_custom_call" | custom-call | tf_op jit(solution)/shard_map/pallas_call | solution.py:437
  91.1 1.4 %copy.13 = bf16[64,256]{1,0:T(8,128)(2,1)} copy(bf16[64,256]{1,0:T(8,128)(2,1)} %shard_map.100) | data formatting | bytes 65536

commit v5 on v4

--- a/solution.py
+++ b/solution.py
@@ -187,22 +187,27 @@
 
         lax.fori_loop(0, front // 32, step, 0)
 
-    def sums_of(at, low, high):
-        total = jnp.dot(matrix[at, :, 0:reach], tables[0, :, low:high], preferred_element_type=f32)
+    def sums_of(at, top, deep, low, high):
+        total = jnp.dot(matrix[at, top : top + deep, 0:reach], tables[0, :, low:high], preferred_element_type=f32)
         for slot in range(1, big_x):
             total = total + jnp.dot(
-                matrix[at, :, slot * reach : (slot + 1) * reach],
+                matrix[at, top : top + deep, slot * reach : (slot + 1) * reach],
                 tables[slot, :, low:high],
                 preferred_element_type=f32,
             )
         return total
 
-    def z_copy(h, s, to):
+    half = front // 2
+    pieces = [(h, 0, front, edges[h], edges[h + 1]) for h in range(halves)]
+    if halves > 1:
+        last = pieces.pop()
+        pieces += [(last[0], r * half, half, last[3], last[4]) for r in range(2)]
+
+    def z_copy(p, s, to):
         peer = {"node": to * big_x + x}
-        cut = pl.ds(edges[h], edges[h + 1] - edges[h])
-        return remote(
-            z_send.at[s, :, cut], z_recv.at[s, :, cut], z_ss.at[h, s], z_rs.at[h, s], peer
-        )
+        _, top, deep, low, high = pieces[p]
+        at = (s, pl.ds(top, deep), pl.ds(low, high - low))
+        return remote(z_send.at[at], z_recv.at[at], z_ss.at[p, s], z_rs.at[p, s], peer)
 
     slots = matrix.shape[0]
     fill(lax.rem(z + 1, big_z) * big_x + x, 0)
@@ -217,25 +222,26 @@
         def _():
             fill(zt * big_x + x, at)
 
-        z_send[s, :, 0 : edges[1]] = sums_of(at, 0, edges[1]).astype(bf16)
+        z_send[s, :, 0 : edges[1]] = sums_of(at, 0, front, 0, edges[1]).astype(bf16)
         z_copy(0, s, zt).start()
         return carry
 
     lax.fori_loop(0, big_z - 1, first_half, 0)
-    for h in range(1, halves):
-        begin = first_copies + (h - 1) * len(x_peers)
-        for copy in table_copies[begin : begin + len(x_peers)]:
-            copy.wait()
-
-        def other_half(s, carry, h=h):
-            low, high = edges[h], edges[h + 1]
-            z_send[s, :, low:high] = sums_of(s, low, high).astype(bf16)
-            z_copy(h, s, lax.rem(z + 1 + s, big_z)).start()
+    for p in range(1, len(pieces)):
+        h, top, deep, low, high = pieces[p]
+        if top == 0:
+            begin = first_copies + (h - 1) * len(x_peers)
+            for copy in table_copies[begin : begin + len(x_peers)]:
+                copy.wait()
+
+        def other_piece(s, carry, p=p, top=top, deep=deep, low=low, high=high):
+            z_send[s, top : top + deep, low:high] = sums_of(s, top, deep, low, high).astype(bf16)
+            z_copy(p, s, lax.rem(z + 1 + s, big_z)).start()
             return carry
 
-        lax.fori_loop(0, big_z - 1, other_half, 0)
+        lax.fori_loop(0, big_z - 1, other_piece, 0)
     fill(node, 0)
-    acc[...] = sums_of(0, 0, width)
+    acc[...] = sums_of(0, 0, front, 0, width)
 
     hidden_part = part.shape[2]
     feats = big_y * CORES
@@ -269,54 +275,62 @@
 
     lax.fori_loop(0, shards * feats, fill_two, 0)
 
-    for h in range(halves):
-        for s in range(big_z - 1):
-            z_copy(h, s, lax.rem(z + 1 + s, big_z)).wait()
-            low, high = edges[h], edges[h + 1]
-            acc[:, low:high] += z_recv[s, :, low:high].astype(f32)
-    mean = (acc[...] / counts_ref[...].astype(f32)).astype(bf16)
-    means[...] = mean
-
-    def part_of(f):
-        at = pl.ds(pl.multiple_of(f * hidden_part, 128), hidden_part)
-        return part[f] + jnp.dot(means[...], pool_one[:, at], preferred_element_type=f32)
-
-    def c_copy(s):
-        return remote(c_send.at[s], c_recv.at[s], c_ss.at[s], c_rs.at[s], c_peer)
-
-    def c_phase(s, carry):
-        yt = lax.rem(y + 1 + s, big_y)
-        c_send[s] = part_of(yt * CORES + other)
-        c_copy(s).start()
-        return carry
-
-    lax.fori_loop(0, big_y, c_phase, 0)
-
-    def y_copy(s, to):
+    def c_copy(r, s):
+        at = (s, pl.ds(r * half, half))
+        return remote(c_send.at[at], c_recv.at[at], c_ss.at[r, s], c_rs.at[r, s], c_peer)
+
+    def y_copy(r, s, to):
         peer = {"feat": to * CORES + core}
-        return remote(y_send.at[s], y_recv.at[s], y_ss.at[s], y_rs.at[s], peer)
-
-    def y_step(s, carry):
-        yt = lax.rem(y + 1 + s, big_y)
-        total = part_of(yt * CORES + core)
-        c_copy(s).wait()
-        total = total + c_recv[s]
-
-        @pl.when(s < big_y - 1)
-        def _():
-            y_send[s] = total.astype(bf16)
-            y_copy(s, yt).start()
-
-        @pl.when(s == big_y - 1)
-        def _():
-            c_send[s] = total
-
-        return carry
-
-    lax.fori_loop(0, big_y, y_step, 0)
+        at = (s, pl.ds(r * half, half))
+        return remote(y_send.at[at], y_recv.at[at], y_ss.at[r, s], y_rs.at[r, s], peer)
+
+    for r in range(2):
+        top, end = r * half, (r + 1) * half
+        for p, (_, first, deep, low, high) in enumerate(pieces):
+            if first == top:
+                for s in range(big_z - 1):
+                    z_copy(p, s, lax.rem(z + 1 + s, big_z)).wait()
+                    acc[first : first + deep, low:high] += z_recv[
+                        s, first : first + deep, low:high
+                    ].astype(f32)
+        means[top:end, :] = (acc[top:end, :] / counts_ref[top:end, :].astype(f32)).astype(bf16)
+
+        def part_of(f, top=top, end=end):
+            at = pl.ds(pl.multiple_of(f * hidden_part, 128), hidden_part)
+            return part[f, top:end, :] + jnp.dot(
+                means[top:end, :], pool_one[:, at], preferred_element_type=f32
+            )
+
+        def c_phase(s, carry, r=r, top=top, end=end, part_of=part_of):
+            yt = lax.rem(y + 1 + s, big_y)
+            c_send[s, top:end, :] = part_of(yt * CORES + other)
+            c_copy(r, s).start()
+            return carry
+
+        lax.fori_loop(0, big_y, c_phase, 0)
+
+        def y_step(s, carry, r=r, top=top, end=end, part_of=part_of):
+            yt = lax.rem(y + 1 + s, big_y)
+            total = part_of(yt * CORES + core)
+            c_copy(r, s).wait()
+            total = total + c_recv[s, top:end, :]
+
+            @pl.when(s < big_y - 1)
+            def _():
+                y_send[s, top:end, :] = total.astype(bf16)
+                y_copy(r, s, yt).start()
+
+            @pl.when(s == big_y - 1)
+            def _():
+                c_send[s, top:end, :] = total
+
+            return carry
+
+        lax.fori_loop(0, big_y, y_step, 0)
     total = c_send[big_y - 1]
     for s in range(big_y - 1):
-        y_copy(s, lax.rem(y + 1 + s, big_y)).wait()
+        for r in range(2):
+            y_copy(r, s, lax.rem(y + 1 + s, big_y)).wait()
         total = total + y_recv[s].astype(f32)
     hidden = jnp.maximum(total, 0.0).astype(bf16)
 
@@ -425,7 +439,7 @@
     hubs = jnp.pad(hub_table, ((0, -hubs_here % 16), (0, 0)))
     reach = rows_here + 128
     edges = (0, 128, 256, width) if width > 256 else (0, width)
-    halves = len(edges) - 1
+    chunks = len(edges) if len(edges) > 2 else 1
     bf16, f32 = jnp.bfloat16, jnp.float32
     dma = pltpu.SemaphoreType.DMA
     zs, xs, ys = big_z - 1, big_x - 1, big_y - 1
@@ -443,7 +457,7 @@
             pltpu.VMEM((shards,) + packed.shape, jnp.int32),
             pltpu.VMEM((shards, front, packed.shape[0]), jnp.int32),
             pltpu.VMEM((big_x, reach, width), bf16),
-            pltpu.VMEM((zs if halves > 1 else 1, front, big_x * reach), bf16),
+            pltpu.VMEM((zs if chunks > 1 else 1, front, big_x * reach), bf16),
             pltpu.VMEM((targets_here * shards, front), bf16),
             pltpu.VMEM((targets_here * shards, 1), f32),
             pltpu.VMEM(block, bf16),
@@ -468,16 +482,16 @@
             pltpu.VMEM((zs, piece, out_width), bf16),
             dma((shards - 1,)),
             dma((shards - 1,)),
-            dma((halves, xs)),
-            dma((halves, xs)),
+            dma((len(edges) - 1, xs)),
+            dma((len(edges) - 1, xs)),
             dma((xs,)),
             dma((xs,)),
-            dma((halves, zs)),
-            dma((halves, zs)),
-            dma((big_y,)),
-            dma((big_y,)),
-            dma((ys,)),
-            dma((ys,)),
+            dma((chunks, zs)),
+            dma((chunks, zs)),
+            dma((2, big_y)),
+            dma((2, big_y)),
+            dma((2, ys)),
+            dma((2, ys)),
             dma((big_y,)),
             dma((big_y,)),
             dma((ys, big_x)),

time: 92.8 us -> 88.5 us (0.954)
  Pallas kernels: 85.6 us -> 81.3 us
    pallas_call x1, Pallas kernels: 85.6 us -> 81.3 us  [body(): pl.pallas_call(functools.partial(main_kernel, (big_z, big_x, big_y, fan_o...]
where the time goes in v5:
time: 88.5 us; the launch traced here: 88.2 us
  Pallas kernels  81.3 us (92%)
  local copies, waits for them, and re-layouts  4.14 us (5%)
  other arithmetic  2.75 us (3%)
    pallas_call x1, Pallas kernels, body(): pl.pallas_call(functools.partial(main_kernel, (big_z, big_x, big_y, fan_o...  81.3 us

profile of v5, /device:TPU:0, one launch (start us, length us, event | category | flops | bytes accessed | tf_op | source)
XLA Modules:
  0.0 88.2 jit_solution(1580201759173628496)
XLA Ops:
  0.0 0.7 select_bitcast_fusion.1
  0.7 0.7 pad_add_fusion.1
  1.4 1.3 %pad.8.hub_ref = bf16[16,512]{1,0:T(8,128)(2,1)} pad(bf16[4,512]{1,0:T(4,128)(2,1)} %param.11, bf16[]{:T(256)} %constant.1.clone.1), padding=0_12x0_0 | pad | bytes 20482 | tf_op jit(solution)/shard_map/jit(_pad)/pad | solution.py:439
  2.7 0.7 select_bitcast_fusion
  3.4 0.6 pad_add_fusion.packed_ref
  4.0 1.5 %broadcast_in_dim.22.counts_ref = s32[384,1]{1,0:T(8,128)} reshape(s32[384]{0:T(512)} %param.17) | data formatting | bytes 3072 | tf_op jit(solution)/shard_map/broadcast_in_dim | solution.py:434
  5.5 81.3 %shard_map.100 = bf16[64,256]{1,0:T(8,128)(2,1)} custom-call(bf16[1024,512]{1,0:T(8,128)(2,1)} %table_ref.1, bf16[16,512]{1,0:T(8,128)(2,1)} %pad.8.hub_ref, bf16[512,2048]{1,0:T(8,128)(2,1)} %self_one.1, bf16[512,2048]{1,0:T(8,128)(2,1)} %pool_one.1, bf16[512,256]{1,0:T(8,128)(2,1)} %self_two.1, bf16[512,256]{1,0:T(8,128)(2,1)} %pool_two.1, ...), custom_call_target="tpu_custom_call" | custom-call | tf_op jit(solution)/shard_map/pallas_call | solution.py:451
  86.8 1.4 %copy.13 = bf16[64,256]{1,0:T(8,128)(2,1)} copy(bf16[64,256]{1,0:T(8,128)(2,1)} %shard_map.100) | data formatting | bytes 65536

commit v6 on v5

--- a/solution.py
+++ b/solution.py
@@ -303,7 +303,7 @@
 
         def c_phase(s, carry, r=r, top=top, end=end, part_of=part_of):
             yt = lax.rem(y + 1 + s, big_y)
-            c_send[s, top:end, :] = part_of(yt * CORES + other)
+            c_send[s, top:end, :] = part_of(yt * CORES + other).astype(bf16)
             c_copy(r, s).start()
             return carry
 
@@ -313,7 +313,7 @@
             yt = lax.rem(y + 1 + s, big_y)
             total = part_of(yt * CORES + core)
             c_copy(r, s).wait()
-            total = total + c_recv[s, top:end, :]
+            total = total + c_recv[s, top:end, :].astype(f32)
 
             @pl.when(s < big_y - 1)
             def _():
@@ -322,12 +322,12 @@
 
             @pl.when(s == big_y - 1)
             def _():
-                c_send[s, top:end, :] = total
+                part[0, top:end, :] = total
 
             return carry
 
         lax.fori_loop(0, big_y, y_step, 0)
-    total = c_send[big_y - 1]
+    total = part[0]
     for s in range(big_y - 1):
         for r in range(2):
             y_copy(r, s, lax.rem(y + 1 + s, big_y)).wait()
@@ -465,8 +465,8 @@
             pltpu.VMEM((zs,) + block, bf16),
             pltpu.VMEM((zs,) + block, bf16),
             pltpu.VMEM((feats,) + hblock, f32),
-            pltpu.VMEM((big_y,) + hblock, f32),
-            pltpu.VMEM((big_y,) + hblock, f32),
+            pltpu.VMEM((big_y,) + hblock, bf16),
+            pltpu.VMEM((big_y,) + hblock, bf16),
             pltpu.VMEM((ys,) + hblock, bf16),
             pltpu.VMEM((ys,) + hblock, bf16),
             pltpu.VMEM((targets_here, out_width), f32),

time: 88.5 us -> 88.2 us (level)
  no operation moved by 1% of the time
where the time goes in v6:
time: 88.2 us; the launch traced here: 87.9 us
  Pallas kernels  81 us (92%)
  local copies, waits for them, and re-layouts  4.14 us (5%)
  other arithmetic  2.75 us (3%)
    pallas_call x1, Pallas kernels, body(): pl.pallas_call(functools.partial(main_kernel, (big_z, big_x, big_y, fan_o...  81 us

profile of v6, /device:TPU:0, one launch (start us, length us, event | category | flops | bytes accessed | tf_op | source)
XLA Modules:
  0.0 87.9 jit_solution(13271768093028883145)
XLA Ops:
  0.0 0.7 select_bitcast_fusion.1
  0.7 0.7 pad_add_fusion.1
  1.4 1.3 %pad.8.hub_ref = bf16[16,512]{1,0:T(8,128)(2,1)} pad(bf16[4,512]{1,0:T(4,128)(2,1)} %param.11, bf16[]{:T(256)} %constant.1.clone.1), padding=0_12x0_0 | pad | bytes 20482 | tf_op jit(solution)/shard_map/jit(_pad)/pad | solution.py:439
  2.7 0.7 select_bitcast_fusion
  3.4 0.6 pad_add_fusion.packed_ref
  4.0 1.5 %broadcast_in_dim.22.counts_ref = s32[384,1]{1,0:T(8,128)} reshape(s32[384]{0:T(512)} %param.17) | data formatting | bytes 3072 | tf_op jit(solution)/shard_map/broadcast_in_dim | solution.py:434
  5.5 81.0 %shard_map.100 = bf16[64,256]{1,0:T(8,128)(2,1)} custom-call(bf16[1024,512]{1,0:T(8,128)(2,1)} %table_ref.1, bf16[16,512]{1,0:T(8,128)(2,1)} %pad.8.hub_ref, bf16[512,2048]{1,0:T(8,128)(2,1)} %self_one.1, bf16[512,2048]{1,0:T(8,128)(2,1)} %pool_one.1, bf16[512,256]{1,0:T(8,128)(2,1)} %self_two.1, bf16[512,256]{1,0:T(8,128)(2,1)} %pool_two.1, ...), custom_call_target="tpu_custom_call" | custom-call | tf_op jit(solution)/shard_map/pallas_call | solution.py:451
  86.5 1.4 %copy.13 = bf16[64,256]{1,0:T(8,128)(2,1)} copy(bf16[64,256]{1,0:T(8,128)(2,1)} %shard_map.100) | data formatting | bytes 65536
